TPU v7x, 32 devices: a whole 2x2x4 slice. The times are simulated.
32 devices in a mesh: section: 2 (over core), dp: 4 (over z), tensor: 4 (over y, x).
Axes of the slice: x: 2, y: 2, z: 4, core: 2. Of those that a mesh axis runs over, the one named last changes fastest.
Arguments:
- inputs: bfloat16 [2, 4096, 768], P(None, ('dp', 'tensor')), may hold values from -6 to 6
- lengths: int32 [2, 4], P(None, 'dp'), may hold values from 1 to 1024, 2457 in all within a row
- cotangent: bfloat16 [2, 4096, 768], P(None, ('dp', 'tensor')), may hold values from -6 to 6
- w_query: bfloat16 [2, 768, 768], P('section', 'dp', 'tensor'), may hold values from -0.21875 to 0.21875
- w_key: bfloat16 [2, 768, 768], P('section', 'dp', 'tensor'), may hold values from -0.21875 to 0.21875
- w_value: bfloat16 [2, 768, 768], P('section', 'dp', 'tensor'), may hold values from -0.21875 to 0.21875
- w_out: bfloat16 [2, 768, 768], P('section', 'dp', 'tensor'), may hold values from -2 to 2
- w_gate: bfloat16 [2, 768, 1152], P('section', 'dp', 'tensor'), may hold values from -0.21875 to 0.21875
- w_up: bfloat16 [2, 768, 1152], P('section', 'dp', 'tensor'), may hold values from -0.21875 to 0.21875
- w_down: bfloat16 [2, 768, 1152], P('section', 'dp', 'tensor'), may hold values from -0.375 to 0.375
- norm_gains: bfloat16 [2, 768, 2], P('section', 'dp'), may hold values from 0.5 to 1.5
Outputs:
- activations: bfloat16 [2, 2, 4096, 768], P('section', None, ('dp', 'tensor'))
- input_grads: bfloat16 [2, 2, 4096, 768], P('section', None, ('dp', 'tensor'))
- grad_query: float32 [2, 768, 768], P('section', 'dp', 'tensor')
- grad_key: float32 [2, 768, 768], P('section', 'dp', 'tensor')
- grad_value: float32 [2, 768, 768], P('section', 'dp', 'tensor')
- grad_out: float32 [2, 768, 768], P('section', 'dp', 'tensor')
- grad_gate: float32 [2, 768, 1152], P('section', 'dp', 'tensor')
- grad_up: float32 [2, 768, 1152], P('section', 'dp', 'tensor')
- grad_down: float32 [2, 768, 1152], P('section', 'dp', 'tensor')
- grad_gains: float32 [2, 768, 2], P('section', 'dp')
Inputs may be any that keep to these rules, and one draw needn't show every extreme that they name: Each micro-batch's lengths sum to 2457 and their largest is exactly 1024; a sequence occupies the first lengths[m, d] positions of its 1024 rows, the rest is padding.
All inputs are finite; a program needn't handle non-finite values. No bound on the sum of `lengths` on one device may be relied on, other than what follows from the above.
Results may differ from a plain program's by a relative error of at most 0.03.
Values may be sent and summed in bfloat16 or wider, within the bound.
No kernel may reach another device: no remote copies, remote signals or barrier semaphores. Data moves between devices by JAX's collectives and lax.ppermute only.
A program may use at most 192 MiB of HBM per device.

v0:
```python
import jax
import jax.numpy as jnp
from jax import lax
from jax.sharding import PartitionSpec as P

HEAD = 64
WINDOW = 128
SLOT = 1024


EPSILON = 1e-05


def from_behind(value, axis, by):
    devices = lax.axis_size(axis)
    pairs = [(i, i + by) for i in range(devices) if 0 <= i + by < devices]
    return lax.ppermute(value, axis, pairs)


def layer_norm(rows, gain):
    centre = rows - jnp.mean(rows, axis=-1, keepdims=True)
    variance = jnp.mean(centre * centre, axis=-1, keepdims=True)
    return centre * lax.rsqrt(variance + EPSILON) * gain


def rotary_tables(count, theta):
    position = jnp.arange(count, dtype=jnp.float32)[:, None]
    index = jnp.arange(HEAD // 2, dtype=jnp.float32)[None, :]
    inverse = jnp.exp(-jnp.log(theta) * (2.0 * index / HEAD))
    angle = position * inverse
    cosine = jnp.concatenate([jnp.cos(angle), jnp.cos(angle)], axis=1)[:, None, :]
    sine = jnp.concatenate([jnp.sin(angle), jnp.sin(angle)], axis=1)[:, None, :]
    return (cosine, sine)


def rotate(heads, cosine, sine):
    half = HEAD // 2
    turned = jnp.concatenate([-heads[..., half:], heads[..., :half]], axis=-1)
    return heads * cosine + turned * sine


def visible(count, half_window, length):
    rows = jnp.arange(count, dtype=jnp.int32)[:, None]
    columns = jnp.arange(count, dtype=jnp.int32)[None, :]
    near = (jnp.abs(rows - columns) <= half_window) & (columns < length)
    return near | (rows == columns)


def unpack(fetched):
    return [weight[0] for weight in fetched]


def attention_scores(q_rot, k_rot, half_window, length):
    count = q_rot.shape[0]
    allowed = visible(count, half_window, length)[None]
    raw = jnp.einsum("qhd,khd->hqk", q_rot, k_rot, preferred_element_type=jnp.float32) * HEAD ** (
        -0.5
    )
    return jnp.where(allowed, raw, -1e30)


def forward_layer(resid, fetched, half_window, theta, length):
    w_query, w_key, w_value, w_out, w_gate, w_up, w_down, gains = unpack(fetched)
    gains = gains.astype(jnp.float32)
    normed = layer_norm(resid, gains[:, 0]).astype(jnp.bfloat16)
    seq_normed = lax.all_gather(normed, "tensor", axis=0, tiled=True)
    count = seq_normed.shape[0]
    heads = w_query.shape[1] // HEAD
    cosine, sine = rotary_tables(count, theta)
    query = jnp.dot(seq_normed, w_query, preferred_element_type=jnp.float32)
    key = jnp.dot(seq_normed, w_key, preferred_element_type=jnp.float32)
    value = jnp.dot(seq_normed, w_value, preferred_element_type=jnp.float32)
    q_rot = rotate(query.reshape(count, heads, HEAD), cosine, sine).astype(jnp.bfloat16)
    k_rot = rotate(key.reshape(count, heads, HEAD), cosine, sine).astype(jnp.bfloat16)
    v_low = value.reshape(count, heads, HEAD).astype(jnp.bfloat16)
    scores = attention_scores(q_rot, k_rot, half_window, length)
    highest = jnp.max(scores, axis=-1, keepdims=True)
    lifted = jnp.exp(scores - highest)
    summed = jnp.sum(lifted, axis=-1, keepdims=True)
    probs_low = (lifted / summed).astype(jnp.bfloat16)
    log_total = highest + jnp.log(summed)
    attended = jnp.einsum("hqk,khd->qhd", probs_low, v_low, preferred_element_type=jnp.float32)
    attended = attended.reshape(count, heads * HEAD).astype(jnp.bfloat16)
    branch = jnp.einsum("sc,dc->sd", attended, w_out, preferred_element_type=jnp.float32)
    mixed = resid + lax.psum_scatter(
        branch.astype(jnp.bfloat16), "tensor", scatter_dimension=0, tiled=True
    ).astype(jnp.float32)
    normed_two = layer_norm(mixed, gains[:, 1]).astype(jnp.bfloat16)
    seq_two = lax.all_gather(normed_two, "tensor", axis=0, tiled=True)
    gate = jnp.dot(seq_two, w_gate, preferred_element_type=jnp.float32)
    upper = jnp.dot(seq_two, w_up, preferred_element_type=jnp.float32)
    hidden = (jax.nn.gelu(gate, approximate=False) * upper).astype(jnp.bfloat16)
    down_term = jnp.einsum("sf,df->sd", hidden, w_down, preferred_element_type=jnp.float32)
    result = mixed + lax.psum_scatter(
        down_term.astype(jnp.bfloat16), "tensor", scatter_dimension=0, tiled=True
    ).astype(jnp.float32)
    return (
        result,
        (seq_normed, q_rot, k_rot, v_low, log_total, attended, mixed, seq_two, gate, upper),
    )


def geglu(gate, upper):
    return jax.nn.gelu(gate, approximate=False) * upper


def backward_layer(grad_out, resid, kept, fetched, half_window, theta, length):
    w_query, w_key, w_value, w_out, w_gate, w_up, w_down, gains = unpack(fetched)
    gains = gains.astype(jnp.float32)
    seq_normed, q_rot, k_rot, v_low, log_total, attended, mixed, seq_two, gate, upper = kept
    count = seq_normed.shape[0]
    heads = w_query.shape[1] // HEAD
    cosine, sine = rotary_tables(count, theta)
    ffn_grad = lax.all_gather(grad_out.astype(jnp.bfloat16), "tensor", axis=0, tiled=True)
    use_gate, use_up, use_down = (w_gate, w_up, w_down)
    hidden = geglu(gate, upper).astype(jnp.bfloat16)
    grad_down = jnp.einsum("sd,sf->df", ffn_grad, hidden, preferred_element_type=jnp.float32)
    d_hidden = jnp.dot(ffn_grad, use_down, preferred_element_type=jnp.float32)
    _, pull_geglu = jax.vjp(geglu, gate, upper)
    d_gate, d_upper = pull_geglu(d_hidden)
    d_gate = d_gate.astype(jnp.bfloat16)
    d_upper = d_upper.astype(jnp.bfloat16)
    grad_gate = jnp.einsum("sd,sf->df", seq_two, d_gate, preferred_element_type=jnp.float32)
    grad_up = jnp.einsum("sd,sf->df", seq_two, d_upper, preferred_element_type=jnp.float32)
    d_two = jnp.einsum("sf,df->sd", d_gate, use_gate, preferred_element_type=jnp.float32)
    d_two = d_two + jnp.einsum("sf,df->sd", d_upper, use_up, preferred_element_type=jnp.float32)
    d_two = lax.psum_scatter(
        d_two.astype(jnp.bfloat16), "tensor", scatter_dimension=0, tiled=True
    ).astype(jnp.float32)
    _, pull_second = jax.vjp(layer_norm, mixed, gains[:, 1])
    d_mixed, gain_two = pull_second(d_two)
    d_mixed = d_mixed + grad_out
    attn_grad = lax.all_gather(d_mixed.astype(jnp.bfloat16), "tensor", axis=0, tiled=True)
    grad_proj = jnp.einsum("sd,sc->dc", attn_grad, attended, preferred_element_type=jnp.float32)
    d_attended = jnp.dot(attn_grad, w_out, preferred_element_type=jnp.float32)
    d_attended = d_attended.astype(jnp.bfloat16).reshape(count, heads, HEAD)
    scores = attention_scores(q_rot, k_rot, half_window, length)
    probs = jnp.exp(scores - log_total)
    d_probs = jnp.einsum("qhd,khd->hqk", d_attended, v_low, preferred_element_type=jnp.float32)
    d_scores = (probs * (d_probs - jnp.sum(probs * d_probs, axis=-1, keepdims=True))).astype(
        jnp.bfloat16
    )
    scale = HEAD ** (-0.5)
    d_query = (
        jnp.einsum("hqk,khd->qhd", d_scores, k_rot, preferred_element_type=jnp.float32) * scale
    )
    d_key = jnp.einsum("hqk,qhd->khd", d_scores, q_rot, preferred_element_type=jnp.float32) * scale
    d_value = jnp.einsum(
        "hqk,qhd->khd", probs.astype(jnp.bfloat16), d_attended, preferred_element_type=jnp.float32
    )
    d_query = rotate(d_query, cosine, -sine).reshape(count, heads * HEAD).astype(jnp.bfloat16)
    d_key = rotate(d_key, cosine, -sine).reshape(count, heads * HEAD).astype(jnp.bfloat16)
    d_value = d_value.reshape(count, heads * HEAD).astype(jnp.bfloat16)
    grad_query = jnp.einsum("sd,sc->dc", seq_normed, d_query, preferred_element_type=jnp.float32)
    grad_key = jnp.einsum("sd,sc->dc", seq_normed, d_key, preferred_element_type=jnp.float32)
    grad_value = jnp.einsum("sd,sc->dc", seq_normed, d_value, preferred_element_type=jnp.float32)
    d_one = jnp.einsum("sc,dc->sd", d_query, w_query, preferred_element_type=jnp.float32)
    d_one = d_one + jnp.einsum("sc,dc->sd", d_key, w_key, preferred_element_type=jnp.float32)
    d_one = d_one + jnp.einsum("sc,dc->sd", d_value, w_value, preferred_element_type=jnp.float32)
    d_one = lax.psum_scatter(
        d_one.astype(jnp.bfloat16), "tensor", scatter_dimension=0, tiled=True
    ).astype(jnp.float32)
    _, pull_first = jax.vjp(layer_norm, resid, gains[:, 0])
    d_resid, gain_one = pull_first(d_one)
    d_resid = d_resid + d_mixed
    gain_grads = jnp.stack([gain_one, gain_two], axis=1)
    return (
        d_resid,
        (grad_query, grad_key, grad_value, grad_proj, grad_gate, grad_up, grad_down, gain_grads),
    )


def fetch_weights(params):
    return (
        lax.all_gather(params[0], "dp", axis=1, tiled=True),
        lax.all_gather(params[1], "dp", axis=1, tiled=True),
        lax.all_gather(params[2], "dp", axis=1, tiled=True),
        lax.all_gather(params[3], "dp", axis=1, tiled=True),
        lax.all_gather(params[4], "dp", axis=1, tiled=True),
        lax.all_gather(params[5], "dp", axis=1, tiled=True),
        lax.all_gather(params[6], "dp", axis=1, tiled=True),
        lax.all_gather(params[7], "dp", axis=1, tiled=True),
    )


def reduce_grads(grads):
    return (
        lax.psum_scatter(
            grads[0].astype(jnp.bfloat16), "dp", scatter_dimension=1, tiled=True
        ).astype(jnp.float32),
        lax.psum_scatter(
            grads[1].astype(jnp.bfloat16), "dp", scatter_dimension=1, tiled=True
        ).astype(jnp.float32),
        lax.psum_scatter(
            grads[2].astype(jnp.bfloat16), "dp", scatter_dimension=1, tiled=True
        ).astype(jnp.float32),
        lax.psum_scatter(
            grads[3].astype(jnp.bfloat16), "dp", scatter_dimension=1, tiled=True
        ).astype(jnp.float32),
        lax.psum_scatter(
            grads[4].astype(jnp.bfloat16), "dp", scatter_dimension=1, tiled=True
        ).astype(jnp.float32),
        lax.psum_scatter(
            grads[5].astype(jnp.bfloat16), "dp", scatter_dimension=1, tiled=True
        ).astype(jnp.float32),
        lax.psum_scatter(
            grads[6].astype(jnp.bfloat16), "dp", scatter_dimension=1, tiled=True
        ).astype(jnp.float32),
        lax.psum_scatter(
            grads[7].astype(jnp.bfloat16), "dp", scatter_dimension=1, tiled=True
        ).astype(jnp.float32),
    )


def local(
    inputs, lengths, cotangent, w_query, w_key, w_value, w_out, w_gate, w_up, w_down, norm_gains
):
    params = (w_query, w_key, w_value, w_out, w_gate, w_up, w_down, norm_gains)
    micro = inputs.shape[0]
    section = lax.axis_index("section")
    first = section == 0
    half_window = jnp.where(first, WINDOW // 2, SLOT).astype(jnp.int32)
    theta = jnp.where(first, 10000.0, 160000.0).astype(jnp.float32)
    outgoing = None
    produced = []
    stored = []
    for tick in range(micro + 1):
        fetched = fetch_weights(params)
        which = jnp.clip(tick - section, 0, micro - 1)
        length = lax.dynamic_index_in_dim(lengths, which, 0, keepdims=False)[0]
        local_input = inputs[min(tick, micro - 1)].astype(jnp.float32)
        if tick == 0:
            arrived = jnp.zeros_like(local_input)
        else:
            arrived = from_behind(outgoing, "section", 1).astype(jnp.float32)
        resid = jnp.where(first, local_input, arrived)
        result, kept = forward_layer(resid, fetched, half_window, theta, length)
        outgoing = result.astype(jnp.bfloat16)
        produced.append(outgoing)
        stored.append((resid,) + kept)
    activations = lax.dynamic_slice_in_dim(jnp.stack(produced), section, micro, 0)[None]
    stacked = jax.tree.map(lambda *items: jnp.stack(items), *stored)
    shard_sums = tuple((jnp.zeros(weight.shape, jnp.float32) for weight in params))
    returning = None
    sent_back = []
    for tick in range(micro + 1):
        fetched = fetch_weights(params)
        target = tick - 1 + section
        live = (target >= 0) & (target < micro)
        which = jnp.clip(target, 0, micro - 1)
        length = lax.dynamic_index_in_dim(lengths, which, 0, keepdims=False)[0]
        local_grad = cotangent[min(tick, micro - 1)].astype(jnp.float32)
        if tick == 0:
            arrived = jnp.zeros_like(local_grad)
        else:
            arrived = from_behind(returning, "section", -1).astype(jnp.float32)
        grad_out = jnp.where(live, jnp.where(first, arrived, local_grad), 0.0)
        slot_index = jnp.clip(tick - 1 + 2 * section, 0, micro)
        kept = jax.tree.map(
            lambda item: lax.dynamic_index_in_dim(item, slot_index, 0, keepdims=False), stacked
        )
        d_resid, grads = backward_layer(
            grad_out, kept[0], kept[1:], fetched, half_window, theta, length
        )
        grads = tuple((grad[None] for grad in grads))
        pieces = reduce_grads(grads)
        shard_sums = tuple((older + newer for older, newer in zip(shard_sums, pieces)))
        returning = d_resid.astype(jnp.bfloat16)
        sent_back.append(returning)
    input_grads = lax.dynamic_slice_in_dim(jnp.stack(sent_back), 1 - section, micro, 0)[None]
    gain_grads = lax.psum(shard_sums[7], "tensor")
    return (
        activations,
        input_grads,
        shard_sums[0],
        shard_sums[1],
        shard_sums[2],
        shard_sums[3],
        shard_sums[4],
        shard_sums[5],
        shard_sums[6],
        gain_grads,
    )


def solution(mesh):
    placed = (
        P(None, ("dp", "tensor"), None),
        P(None, "dp"),
        P(None, ("dp", "tensor"), None),
        P("section", "dp", "tensor"),
        P("section", "dp", "tensor"),
        P("section", "dp", "tensor"),
        P("section", "dp", "tensor"),
        P("section", "dp", "tensor"),
        P("section", "dp", "tensor"),
        P("section", "dp", "tensor"),
        P("section", "dp", None),
    )
    return jax.shard_map(
        local,
        mesh=mesh,
        in_specs=placed,
        out_specs=(
            P("section", None, ("dp", "tensor"), None),
            P("section", None, ("dp", "tensor"), None),
            P("section", "dp", "tensor"),
            P("section", "dp", "tensor"),
            P("section", "dp", "tensor"),
            P("section", "dp", "tensor"),
            P("section", "dp", "tensor"),
            P("section", "dp", "tensor"),
            P("section", "dp", "tensor"),
            P("section", "dp", None),
        ),
        check_vma=False,
    )
```

profile of v0, /device:TPU:0, one launch (start us, length us, event | category | flops | bytes accessed | tf_op | source)
XLA Modules:
  0.0 1628.8 jit_solution(6911992825567047067)
XLA Ops:
  112.9 32.8 %reduce-scatter.85.cloned.1.call-done = bf16[256,768]{1,0:T(8,128)(2,1)} async-done(((bf16[1024,768]{1,0:T(8,128)(2,1)}), bf16[256,768]{1,0:T(8,128)(2,1)}) %reduce-scatter.85.cloned.1.call-update) | async-done | bytes 393232 | tf_op jit(solution)/shard_map/reduce_scatter | solution.py:85
  208.6 31.3 %reduce-scatter.87.cloned.1.call-done = bf16[256,768]{1,0:T(8,128)(2,1)} async-done(((bf16[1024,768]{1,0:T(8,128)(2,1)}), bf16[256,768]{1,0:T(8,128)(2,1)}) %reduce-scatter.87.cloned.1.call-update) | async-done | bytes 393232 | tf_op jit(solution)/shard_map/reduce_scatter | solution.py:94
  249.1 28.2 %all-gather.17.cloned.1.call-done = bf16[1024,768]{1,0:T(8,128)(2,1)} async-done(((bf16[256,768]{1,0:T(8,128)(2,1)}), bf16[1024,768]{1,0:T(8,128)(2,1)}) %all-gather.17.cloned.1.call-update) | async-done | bytes 1572880 | tf_op jit(solution)/shard_map/all_gather | solution.py:66
  299.2 31.2 %reduce-scatter.89.cloned.1.call-done = bf16[256,768]{1,0:T(8,128)(2,1)} async-done(((bf16[1024,768]{1,0:T(8,128)(2,1)}), bf16[256,768]{1,0:T(8,128)(2,1)}) %reduce-scatter.89.cloned.1.call-update) | async-done | bytes 393232 | tf_op jit(solution)/shard_map/reduce_scatter | solution.py:85
  332.9 30.9 %all-gather.19.cloned.1.call-done = bf16[1024,768]{1,0:T(8,128)(2,1)} async-done(((bf16[256,768]{1,0:T(8,128)(2,1)}), bf16[1024,768]{1,0:T(8,128)(2,1)}) %all-gather.19.cloned.1.call-update) | async-done | bytes 1572880 | tf_op jit(solution)/shard_map/all_gather | solution.py:89
  372.7 31.2 %reduce-scatter.91.cloned.1.call-done = bf16[256,768]{1,0:T(8,128)(2,1)} async-done(((bf16[1024,768]{1,0:T(8,128)(2,1)}), bf16[256,768]{1,0:T(8,128)(2,1)}) %reduce-scatter.91.cloned.1.call-update) | async-done | bytes 393232 | tf_op jit(solution)/shard_map/reduce_scatter | solution.py:94
  413.0 28.2 %all-gather.21.cloned.1.call-done = bf16[1024,768]{1,0:T(8,128)(2,1)} async-done(((bf16[256,768]{1,0:T(8,128)(2,1)}), bf16[1024,768]{1,0:T(8,128)(2,1)}) %all-gather.21.cloned.1.call-update) | async-done | bytes 1572880 | tf_op jit(solution)/shard_map/all_gather | solution.py:66
  463.1 31.2 %reduce-scatter.93.cloned.1.call-done = bf16[256,768]{1,0:T(8,128)(2,1)} async-done(((bf16[1024,768]{1,0:T(8,128)(2,1)}), bf16[256,768]{1,0:T(8,128)(2,1)}) %reduce-scatter.93.cloned.1.call-update) | async-done | bytes 393232 | tf_op jit(solution)/shard_map/reduce_scatter | solution.py:85
  498.6 29.8 %all-gather.23.cloned.1.call-done = bf16[1024,768]{1,0:T(8,128)(2,1)} async-done(((bf16[256,768]{1,0:T(8,128)(2,1)}), bf16[1024,768]{1,0:T(8,128)(2,1)}) %all-gather.23.cloned.1.call-update) | async-done | bytes 1572880 | tf_op jit(solution)/shard_map/all_gather | solution.py:89
  538.1 22.8 %all-gather.25.cloned.1.call-done = bf16[1024,768]{1,0:T(8,128)(2,1)} async-done(((bf16[256,768]{1,0:T(8,128)(2,1)}), bf16[1024,768]{1,0:T(8,128)(2,1)}) %all-gather.25.cloned.1.call-update) | async-done | bytes 1572880 | tf_op jit(solution)/shard_map/all_gather | solution.py:114
  574.3 29.0 %reduce-scatter.97.cloned.1.call-done = bf16[256,768]{1,0:T(8,128)(2,1)} async-done(((bf16[1024,768]{1,0:T(8,128)(2,1)}), bf16[256,768]{1,0:T(8,128)(2,1)}) %reduce-scatter.97.cloned.1.call-update) | async-done | bytes 393232 | tf_op jit(solution)/shard_map/reduce_scatter | solution.py:127
  678.6 28.7 %reduce-scatter.99.cloned.1.call-done = bf16[256,768]{1,0:T(8,128)(2,1)} async-done(((bf16[1024,768]{1,0:T(8,128)(2,1)}), bf16[256,768]{1,0:T(8,128)(2,1)}) %reduce-scatter.99.cloned.1.call-update) | async-done | bytes 393232 | tf_op jit(solution)/shard_map/reduce_scatter | solution.py:160
  718.1 30.8 %all-gather.29.cloned.1.call-done = bf16[1024,768]{1,0:T(8,128)(2,1)} async-done(((bf16[256,768]{1,0:T(8,128)(2,1)}), bf16[1024,768]{1,0:T(8,128)(2,1)}) %all-gather.29.cloned.1.call-update) | async-done | bytes 1572880 | tf_op jit(solution)/shard_map/all_gather | solution.py:114
  760.5 31.2 %reduce-scatter.101.cloned.1.call-done = bf16[256,768]{1,0:T(8,128)(2,1)} async-done(((bf16[1024,768]{1,0:T(8,128)(2,1)}), bf16[256,768]{1,0:T(8,128)(2,1)}) %reduce-scatter.101.cloned.1.call-update) | async-done | bytes 393232 | tf_op jit(solution)/shard_map/reduce_scatter | solution.py:127
  808.7 20.6 %all-gather.31.cloned.1.call-done = bf16[1024,768]{1,0:T(8,128)(2,1)} async-done(((bf16[256,768]{1,0:T(8,128)(2,1)}), bf16[1024,768]{1,0:T(8,128)(2,1)}) %all-gather.31.cloned.1.call-update) | async-done | bytes 1572880 | tf_op jit(solution)/shard_map/all_gather | solution.py:133
  868.9 31.2 %reduce-scatter.103.cloned.1.call-done = bf16[256,768]{1,0:T(8,128)(2,1)} async-done(((bf16[1024,768]{1,0:T(8,128)(2,1)}), bf16[256,768]{1,0:T(8,128)(2,1)}) %reduce-scatter.103.cloned.1.call-update) | async-done | bytes 393232 | tf_op jit(solution)/shard_map/reduce_scatter | solution.py:160
  910.1 30.5 %all-gather.33.cloned.1.call-done = bf16[1024,768]{1,0:T(8,128)(2,1)} async-done(((bf16[256,768]{1,0:T(8,128)(2,1)}), bf16[1024,768]{1,0:T(8,128)(2,1)}) %all-gather.33.cloned.1.call-update) | async-done | bytes 1572880 | tf_op jit(solution)/shard_map/all_gather | solution.py:114
  1227.5 21.2 %reduce-scatter.135.cloned.1.call-done = bf16[192,288]{1,0:T(8,128)(2,1)} async-done(((bf16[768,288]{1,0:T(8,128)(2,1)}), bf16[192,288]{1,0:T(8,128)(2,1)}) %reduce-scatter.135.cloned.1.call-update) | async-done | bytes 110608
  1295.5 20.3 %reduce-scatter.111.cloned.1.call-done = bf16[192,192]{1,0:T(8,128)(2,1)} async-done(((bf16[768,192]{1,0:T(8,128)(2,1)}), bf16[192,192]{1,0:T(8,128)(2,1)}) %reduce-scatter.111.cloned.1.call-update) | async-done | bytes 73744
  1359.3 20.1 %reduce-scatter.129.cloned.1.call-done = bf16[192,192]{1,0:T(8,128)(2,1)} async-done(((bf16[768,192]{1,0:T(8,128)(2,1)}), bf16[192,192]{1,0:T(8,128)(2,1)}) %reduce-scatter.129.cloned.1.call-update) | async-done | bytes 73744
  1401.5 21.2 %reduce-scatter.137.cloned.1.call-done = bf16[192,288]{1,0:T(8,128)(2,1)} async-done(((bf16[768,288]{1,0:T(8,128)(2,1)}), bf16[192,288]{1,0:T(8,128)(2,1)}) %reduce-scatter.137.cloned.1.call-update) | async-done | bytes 110608
  1425.0 20.6 %reduce-scatter.143.cloned.1.call-done = bf16[192,288]{1,0:T(8,128)(2,1)} async-done(((bf16[768,288]{1,0:T(8,128)(2,1)}), bf16[192,288]{1,0:T(8,128)(2,1)}) %reduce-scatter.143.cloned.1.call-update) | async-done | bytes 110608
  1447.8 20.5 %reduce-scatter.149.cloned.1.call-done = bf16[192,288]{1,0:T(8,128)(2,1)} async-done(((bf16[768,288]{1,0:T(8,128)(2,1)}), bf16[192,288]{1,0:T(8,128)(2,1)}) %reduce-scatter.149.cloned.1.call-update) | async-done | bytes 110608
  1555.3 30.3 %reduce-scatter.107.cloned.1.call-done = bf16[256,768]{1,0:T(8,128)(2,1)} async-done(((bf16[1024,768]{1,0:T(8,128)(2,1)}), bf16[256,768]{1,0:T(8,128)(2,1)}) %reduce-scatter.107.cloned.1.call-update) | async-done | bytes 393232 | tf_op jit(solution)/shard_map/reduce_scatter | solution.py:160
  (947 shorter events, 956.8 us)
Async XLA Ops:
  951.9 141.8 %reduce-scatter.133.cloned.1.call-start = ((), (), s32[]{:S(2)}) async-start(), calls=%async_computation.72 | async-start | bytes 737280
  965.0 132.2 %reduce-scatter.139.cloned.1.call-start = ((), (), s32[]{:S(2)}) async-start(), calls=%async_computation.75 | async-start | bytes 737280
  997.3 132.8 %reduce-scatter.115.cloned.1.call-start = ((), (), s32[]{:S(2)}) async-start(), calls=%async_computation.63 | async-start | bytes 491520
  1000.7 160.2 %all-gather.35.cloned.1.call-start = ((), (), s32[]{:S(2)}) async-start(), calls=%async_computation.58 | async-start | bytes 1966080 | tf_op jit(solution)/shard_map/all_gather | solution.py:133
  1005.2 185.6 %reduce-scatter.121.cloned.1.call-start = ((), (), s32[]{:S(2)}) async-start(), calls=%async_computation.66 | async-start | bytes 491520
  1008.6 196.6 %reduce-scatter.127.cloned.1.call-start = ((), (), s32[]{:S(2)}) async-start(), calls=%async_computation.69 | async-start | bytes 491520
  1012.6 213.4 %reduce-scatter.151.cloned.1.call-start = ((), (), s32[]{:S(2)}) async-start(), calls=%async_computation.81 | async-start | bytes 245760
  1013.8 234.8 %reduce-scatter.135.cloned.1.call-start = ((), (), s32[]{:S(2)}) async-start(), calls=%async_computation.73 | async-start | bytes 737280
  1018.2 253.2 %reduce-scatter.141.cloned.1.call-start = ((), (), s32[]{:S(2)}) async-start(), calls=%async_computation.76 | async-start | bytes 737280
  1028.2 266.1 %reduce-scatter.147.cloned.1.call-start = ((), (), s32[]{:S(2)}) async-start(), calls=%async_computation.79 | async-start | bytes 737280
  1038.7 277.2 %reduce-scatter.111.cloned.1.call-start = ((), (), s32[]{:S(2)}) async-start(), calls=%async_computation.61 | async-start | bytes 491520
  1046.3 290.6 %reduce-scatter.117.cloned.1.call-start = ((), (), s32[]{:S(2)}) async-start(), calls=%async_computation.64 | async-start | bytes 491520
  1054.0 304.1 %reduce-scatter.123.cloned.1.call-start = ((), (), s32[]{:S(2)}) async-start(), calls=%async_computation.67 | async-start | bytes 491520
  1061.7 317.7 %reduce-scatter.129.cloned.1.call-start = ((), (), s32[]{:S(2)}) async-start(), calls=%async_computation.70 | async-start | bytes 491520
  1070.1 329.9 %reduce-scatter.153.cloned.1.call-start = ((), (), s32[]{:S(2)}) async-start(), calls=%async_computation.82 | async-start | bytes 245760
  1075.8 346.9 %reduce-scatter.137.cloned.1.call-start = ((), (), s32[]{:S(2)}) async-start(), calls=%async_computation.74 | async-start | bytes 737280
  1085.7 359.9 %reduce-scatter.143.cloned.1.call-start = ((), (), s32[]{:S(2)}) async-start(), calls=%async_computation.77 | async-start | bytes 737280
  1114.1 354.2 %reduce-scatter.149.cloned.1.call-start = ((), (), s32[]{:S(2)}) async-start(), calls=%async_computation.80 | async-start | bytes 737280
  1141.4 348.3 %reduce-scatter.113.cloned.1.call-start = ((), (), s32[]{:S(2)}) async-start(), calls=%async_computation.62 | async-start | bytes 491520
  1190.7 320.3 %reduce-scatter.119.cloned.1.call-start = ((), (), s32[]{:S(2)}) async-start(), calls=%async_computation.65 | async-start | bytes 491520
  1254.0 278.2 %reduce-scatter.125.cloned.1.call-start = ((), (), s32[]{:S(2)}) async-start(), calls=%async_computation.68 | async-start | bytes 491520
  1264.2 289.1 %reduce-scatter.131.cloned.1.call-start = ((), (), s32[]{:S(2)}) async-start(), calls=%async_computation.71 | async-start | bytes 491520
  1277.2 308.3 %reduce-scatter.107.cloned.1.call-start = ((), (), s32[]{:S(2)}) async-start(), calls=%async_computation.59 | async-start | bytes 1966080 | tf_op jit(solution)/shard_map/reduce_scatter | solution.py:160
  1281.1 329.6 %reduce-scatter.155.cloned.1.call-start = ((), (), s32[]{:S(2)}) async-start(), calls=%async_computation.83 | async-start | bytes 245760
  (258 other events, 4735.3 us)
Sparse Core Ops, SparseCore 0:
  27.5 32.5 all-gather.12
  113.0 32.6 reduce-scatter.84
  150.2 30.8 all-gather.14
  208.7 31.1 reduce-scatter.86
  246.3 30.8 all-gather.16
  299.2 31.0 reduce-scatter.88
  333.0 30.8 all-gather.18
  372.8 31.1 reduce-scatter.90
  410.3 30.8 all-gather.20
  463.2 31.1 reduce-scatter.92
  497.5 30.8 all-gather.22
  530.1 30.8 all-gather.24
  572.1 31.1 reduce-scatter.96
  607.9 30.8 all-gather.26
  676.0 31.1 reduce-scatter.98
  718.0 30.8 all-gather.28
  760.5 31.1 reduce-scatter.100
  798.5 30.8 all-gather.30
  868.9 31.1 reduce-scatter.102
  909.7 30.8 all-gather.32
  952.0 31.1 reduce-scatter.104
  1056.3 29.5 reduce-scatter.94
  1131.8 29.0 all-gather.34
  1556.2 29.3 reduce-scatter.106
  (24 shorter events, 472.0 us)
where the time goes:
time: 1650 us; the launch traced here: 1630 us
  waiting for transfers between devices  913 us (55%)
  matrix products  241 us (15%)
  local copies, waits for them, and re-layouts  185 us (11%)
  blocking collectives  136 us (8%)
  other arithmetic  126 us (8%)
  between operations  18.1 us (1%)
    unnamed x72, waiting for transfers between devices  339 us
    unnamed x564, local copies, waits for them, and re-layouts  182 us
    reduce_scatter x3, waiting for transfers between devices, forward_layer(): lax.psum_scatter(branch.astype(jnp.bfloat16), 'tensor', scatter_dimension...  95.3 us
    reduce_scatter x3, waiting for transfers between devices, backward_layer(): lax.psum_scatter(d_one.astype(jnp.bfloat16), 'tensor', scatter_dimension=...  90.2 us
    all_gather x3, waiting for transfers between devices, backward_layer(): lax.all_gather(grad_out.astype(jnp.bfloat16), 'tensor', axis=0, tiled=True)  84.1 us
    reduce_scatter x3, waiting for transfers between devices, forward_layer(): lax.psum_scatter(down_term.astype(jnp.bfloat16), 'tensor', scatter_dimens...  62.5 us
    all_gather x3, waiting for transfers between devices, forward_layer(): seq_two = lax.all_gather(normed_two, 'tensor', axis=0, tiled=True)  60.7 us
    reduce_scatter x3, waiting for transfers between devices, backward_layer(): lax.psum_scatter(d_two.astype(jnp.bfloat16), 'tensor', scatter_dimension=...  60.3 us
  transfers between devices with their start and end apart: 52, of which 43 were waited for; matrix products, arithmetic and copies ran while one was open for 18% of the time, Pallas kernels for 0%

commit v1 on v0

v1 whole, which is shorter than its diff:
```python
import functools

import jax
import jax.numpy as jnp
from jax import lax
from jax.experimental import pallas as pl
from jax.experimental.pallas import tpu as pltpu
from jax.sharding import PartitionSpec as P

HEAD = 64
HALF_WINDOW = 64
THETAS = (10000.0, 160000.0)
EPSILON = 1e-05
SCALE = HEAD ** (-0.5)
MASKED = -1e30
BF16 = jnp.bfloat16
F32 = jnp.float32
NT = (((1,), (1,)), ((), ()))


def layer_norm(rows, gain):
    centre = rows - jnp.mean(rows, axis=-1, keepdims=True)
    variance = jnp.mean(centre * centre, axis=-1, keepdims=True)
    return centre * lax.rsqrt(variance + EPSILON) * gain


def geglu(gate, upper):
    return jax.nn.gelu(gate, approximate=False) * upper


def exchange(value, by):
    count = lax.axis_size("tensor")
    return lax.ppermute(value, "tensor", [(i, i ^ by) for i in range(count)])


def gather_rows(rows):
    count = lax.axis_size("tensor")
    return jnp.concatenate([rows] + [exchange(rows, by) for by in range(1, count)], axis=0)


def scatter_rows(partial):
    count = lax.axis_size("tensor")
    own = partial.shape[0] // count
    total = partial[:own].astype(F32)
    for by in range(1, count):
        total = total + exchange(partial[by * own : (by + 1) * own], by).astype(F32)
    return total


def positions(own, devices):
    index = lax.axis_index("tensor")
    row = jnp.arange(own * devices, dtype=jnp.int32)
    return ((row // own) ^ index) * own + row % own


def rotary_tables(position, theta):
    index = jnp.arange(HEAD // 2, dtype=F32)[None, :]
    inverse = jnp.exp(-jnp.log(F32(theta)) * (2.0 * index / HEAD))
    angle = position.astype(F32)[:, None] * inverse
    cosine = jnp.cos(angle)
    sine = jnp.sin(angle)
    return (
        jnp.concatenate([cosine, cosine], axis=1),
        jnp.concatenate([sine, sine], axis=1),
    )


def turn(rows):
    half = HEAD // 2
    return jnp.concatenate([-rows[:, half:], rows[:, :half]], axis=1)


def neighbours(scalars, block, own, devices):
    index = scalars[0]
    place = index ^ block
    before = (jnp.maximum(place - 1, 0) ^ index) * own + own - HALF_WINDOW
    after = (jnp.minimum(place + 1, devices - 1) ^ index) * own
    return place, pl.multiple_of(before, HALF_WINDOW), pl.multiple_of(after, HALF_WINDOW)


def attend_kernel(scalars, qkv, cosine, sine, q3, k3, v3, out, lse, *, local, own, devices, heads):
    count = own * devices
    width = heads * HEAD
    length = scalars[1]
    for head in range(heads):
        at = head * HEAD
        for part, store in ((0, q3), (1, k3)):
            rows = qkv[:, part * width + at : part * width + at + HEAD]
            store[head] = (rows * cosine[...] + turn(rows) * sine[...]).astype(BF16)
        v3[head] = qkv[:, 2 * width + at : 2 * width + at + HEAD].astype(BF16)
    for head in range(heads):

        def step(block, carry):
            start = pl.multiple_of(block * own, own)
            query = q3[head, pl.ds(start, own), :]
            if local:
                place, before, after = neighbours(scalars, block, own, devices)
                key = jnp.concatenate(
                    [
                        k3[head, pl.ds(before, HALF_WINDOW), :],
                        k3[head, pl.ds(start, own), :],
                        k3[head, pl.ds(after, HALF_WINDOW), :],
                    ],
                    axis=0,
                )
                value = jnp.concatenate(
                    [
                        v3[head, pl.ds(before, HALF_WINDOW), :],
                        v3[head, pl.ds(start, own), :],
                        v3[head, pl.ds(after, HALF_WINDOW), :],
                    ],
                    axis=0,
                )
                span = own + 2 * HALF_WINDOW
                shape = (own, span)
                row = lax.broadcasted_iota(jnp.int32, shape, 0)
                column = lax.broadcasted_iota(jnp.int32, shape, 1) - HALF_WINDOW
                spot = column + place * own
                near = jnp.abs(row - column) <= HALF_WINDOW
                allowed = (near & (spot >= 0) & (spot < length)) | (row == column)
            else:
                key = k3[head]
                value = v3[head]
                shape = (own, count)
                row = lax.broadcasted_iota(jnp.int32, shape, 0) + start
                column = lax.broadcasted_iota(jnp.int32, shape, 1)
                spot = ((column // own) ^ scalars[0]) * own + column % own
                allowed = (spot < length) | (row == column)
            raw = lax.dot_general(query, key, NT, preferred_element_type=F32) * SCALE
            scores = jnp.where(allowed, raw, MASKED)
            highest = jnp.max(scores, axis=1, keepdims=True)
            lifted = jnp.exp(scores - highest)
            summed = jnp.sum(lifted, axis=1, keepdims=True)
            probs = (lifted / summed).astype(BF16)
            got = jnp.dot(probs, value, preferred_element_type=F32)
            out[pl.ds(start, own), head * HEAD : (head + 1) * HEAD] = got.astype(BF16)
            total = jnp.broadcast_to(highest + jnp.log(summed), (own, 128))
            lse[head, :, pl.ds(start, own)] = total.T[:8]
            return carry

        lax.fori_loop(0, devices, step, 0)


def attend(qkv, cosine, sine, scalars, local, own, devices, heads):
    count = own * devices
    split = jax.ShapeDtypeStruct((heads, count, HEAD), BF16)
    vmem = pl.BlockSpec(memory_space=pltpu.VMEM)
    return pl.pallas_call(
        functools.partial(attend_kernel, local=local, own=own, devices=devices, heads=heads),
        out_shape=(
            split,
            split,
            split,
            jax.ShapeDtypeStruct((count, heads * HEAD), BF16),
            jax.ShapeDtypeStruct((heads, 8, count), F32),
        ),
        in_specs=[pl.BlockSpec(memory_space=pltpu.SMEM), vmem, vmem, vmem],
        out_specs=(vmem, vmem, vmem, vmem, vmem),
        name="attend",
    )(scalars, qkv, cosine, sine)


def attend_back_kernel(
    scalars, q3, k3, v3, grad, lse, cosine, sine, out, dk, dv, *, local, own, devices, heads
):
    count = own * devices
    width = heads * HEAD
    length = scalars[1]
    for head in range(heads):
        dk[...] = jnp.zeros_like(dk)
        dv[...] = jnp.zeros_like(dv)

        def step(block, carry):
            start = pl.multiple_of(block * own, own)
            here = pl.ds(start, own)
            query = q3[head, here, :]
            upstream = grad[here, head * HEAD : (head + 1) * HEAD]
            if local:
                place, before, after = neighbours(scalars, block, own, devices)
                pieces = (
                    (pl.ds(before, HALF_WINDOW), 0, HALF_WINDOW),
                    (here, HALF_WINDOW, HALF_WINDOW + own),
                    (pl.ds(after, HALF_WINDOW), HALF_WINDOW + own, 2 * HALF_WINDOW + own),
                )
                key = jnp.concatenate([k3[head, piece, :] for piece, _, _ in pieces], axis=0)
                value = jnp.concatenate([v3[head, piece, :] for piece, _, _ in pieces], axis=0)
                shape = (own + 2 * HALF_WINDOW, own)
                row = lax.broadcasted_iota(jnp.int32, shape, 1)
                column = lax.broadcasted_iota(jnp.int32, shape, 0) - HALF_WINDOW
                spot = column + place * own
                near = jnp.abs(row - column) <= HALF_WINDOW
                allowed = (near & (spot >= 0) & (spot < length)) | (row == column)
            else:
                pieces = ((slice(None), 0, count),)
                key = k3[head]
                value = v3[head]
                shape = (count, own)
                row = lax.broadcasted_iota(jnp.int32, shape, 1) + start
                column = lax.broadcasted_iota(jnp.int32, shape, 0)
                spot = ((column // own) ^ scalars[0]) * own + column % own
                allowed = (spot < length) | (row == column)
            raw = lax.dot_general(key, query, NT, preferred_element_type=F32) * SCALE
            scores = jnp.where(allowed, raw, MASKED)
            probs = jnp.exp(scores - lse[head, 0:1, here])
            d_probs = lax.dot_general(value, upstream, NT, preferred_element_type=F32)
            weighted = jnp.sum(probs * d_probs, axis=0, keepdims=True)
            d_scores = (probs * (d_probs - weighted)).astype(BF16)
            d_key = jnp.dot(d_scores, query, preferred_element_type=F32) * SCALE
            d_value = jnp.dot(probs.astype(BF16), upstream, preferred_element_type=F32)
            for piece, low, high in pieces:
                dk[piece, :] += d_key[low:high]
                dv[piece, :] += d_value[low:high]
            d_query = jnp.dot(key.T, d_scores, preferred_element_type=F32).T * SCALE
            d_query = d_query * cosine[here, :] - turn(d_query) * sine[here, :]
            out[here, head * HEAD : (head + 1) * HEAD] = d_query.astype(BF16)
            return carry

        lax.fori_loop(0, devices, step, 0)
        at = head * HEAD
        d_key = dk[...] * cosine[...] - turn(dk[...]) * sine[...]
        out[:, width + at : width + at + HEAD] = d_key.astype(BF16)
        out[:, 2 * width + at : 2 * width + at + HEAD] = dv[...].astype(BF16)


def attend_back(q3, k3, v3, grad, lse, cosine, sine, scalars, local, own, devices, heads):
    count = own * devices
    vmem = pl.BlockSpec(memory_space=pltpu.VMEM)
    return pl.pallas_call(
        functools.partial(attend_back_kernel, local=local, own=own, devices=devices, heads=heads),
        out_shape=jax.ShapeDtypeStruct((count, 3 * heads * HEAD), BF16),
        in_specs=[pl.BlockSpec(memory_space=pltpu.SMEM)] + [vmem] * 7,
        out_specs=vmem,
        scratch_shapes=[pltpu.VMEM((count, HEAD), F32), pltpu.VMEM((count, HEAD), F32)],
        name="attend_back",
    )(scalars, q3, k3, v3, grad, lse, cosine, sine)


def forward_layer(resid, weights, gains, local, tables, scalars):
    w_qkv, w_out, w_in, w_down = weights
    own = resid.shape[0]
    devices = lax.axis_size("tensor")
    heads = w_out.shape[1] // HEAD
    rows_one = gather_rows(layer_norm(resid, gains[0]).astype(BF16))
    qkv = jnp.dot(rows_one, w_qkv, preferred_element_type=F32)
    q3, k3, v3, attended, lse = attend(qkv, *tables, scalars, local, own, devices, heads)
    branch = lax.dot_general(attended, w_out, NT, preferred_element_type=F32)
    mixed = resid + scatter_rows(branch.astype(BF16))
    rows_two = gather_rows(layer_norm(mixed, gains[1]).astype(BF16))
    both = jnp.dot(rows_two, w_in, preferred_element_type=F32)
    units = w_down.shape[1]
    hidden = geglu(both[:, :units], both[:, units:]).astype(BF16)
    down = lax.dot_general(hidden, w_down, NT, preferred_element_type=F32)
    result = mixed + scatter_rows(down.astype(BF16))
    return result, (rows_one, q3, k3, v3, lse, attended, mixed, rows_two, both, hidden)


def backward_layer(grad_out, resid, kept, weights, gains, local, tables, scalars):
    w_qkv, w_out, w_in, w_down = weights
    rows_one, q3, k3, v3, lse, attended, mixed, rows_two, both, hidden = kept
    own = resid.shape[0]
    devices = lax.axis_size("tensor")
    heads = w_out.shape[1] // HEAD
    units = w_down.shape[1]
    outer = functools.partial(jnp.einsum, "sd,sf->df", preferred_element_type=F32)
    grad_rows = gather_rows(grad_out.astype(BF16))
    d_hidden = jnp.dot(grad_rows, w_down, preferred_element_type=F32)
    _, pull_geglu = jax.vjp(geglu, both[:, :units], both[:, units:])
    d_both = jnp.concatenate([part.astype(BF16) for part in pull_geglu(d_hidden)], axis=1)
    d_two = lax.dot_general(d_both, w_in, NT, preferred_element_type=F32)
    d_two = scatter_rows(d_two.astype(BF16))
    grad_mlp = jnp.concatenate(
        [outer(rows_two, d_both).astype(BF16), outer(grad_rows, hidden).astype(BF16)], axis=1
    )
    _, pull_second = jax.vjp(layer_norm, mixed, gains[1])
    d_mixed, gain_two = pull_second(d_two)
    d_mixed = d_mixed + grad_out
    mixed_rows = gather_rows(d_mixed.astype(BF16))
    d_attended = jnp.dot(mixed_rows, w_out, preferred_element_type=F32).astype(BF16)
    d_qkv = attend_back(
        q3, k3, v3, d_attended, lse, *tables, scalars, local, own, devices, heads
    )
    d_one = lax.dot_general(d_qkv, w_qkv, NT, preferred_element_type=F32)
    d_one = scatter_rows(d_one.astype(BF16))
    grad_attn = jnp.concatenate(
        [outer(rows_one, d_qkv).astype(BF16), outer(mixed_rows, attended).astype(BF16)], axis=1
    )
    _, pull_first = jax.vjp(layer_norm, resid, gains[0])
    d_resid, gain_one = pull_first(d_one)
    return d_resid + d_mixed, grad_attn, grad_mlp, jnp.stack([gain_one, gain_two])


def reduce_pack(pack):
    half = pack.shape[1] // 2
    halves = jnp.concatenate([pack[:, :half], pack[:, half:]], axis=0)
    return lax.psum_scatter(halves, ("section", "dp"), scatter_dimension=0, tiled=True)


def local_program(
    inputs, lengths, cotangent, w_query, w_key, w_value, w_out, w_gate, w_up, w_down, norm_gains
):
    section = lax.axis_index("section")
    first = section == 0
    devices = lax.axis_size("tensor")
    own = inputs.shape[1]
    features = inputs.shape[2]
    head_width = w_query.shape[2]
    units = w_gate.shape[2]
    swap = functools.partial(lax.ppermute, axis_name="section", perm=[(0, 1), (1, 0)])

    attn_pack = jnp.concatenate([w_query, w_key, w_value, w_out, norm_gains], axis=2)[0]
    mlp_pack = jnp.concatenate([w_gate, w_up, w_down], axis=2)[0]
    attn_all = lax.all_gather(attn_pack, ("section", "dp"), axis=0, tiled=True)
    mlp_all = lax.all_gather(mlp_pack, ("section", "dp"), axis=0, tiled=True)
    weights = []
    gains = []
    for layer in range(2):
        attn = attn_all[layer * features : (layer + 1) * features]
        mlp = mlp_all[layer * features : (layer + 1) * features]
        weights.append(
            (
                attn[:, : 3 * head_width],
                attn[:, 3 * head_width : 4 * head_width],
                mlp[:, : 2 * units],
                mlp[:, 2 * units :],
            )
        )
        gains.append(attn[:, 4 * head_width :].astype(F32).T)

    position = positions(own, devices)
    tables = [rotary_tables(position, theta) for theta in THETAS]
    length = lax.dynamic_index_in_dim(lengths, section, 0, keepdims=False)[0]
    scalars = jnp.stack([lax.axis_index("tensor").astype(jnp.int32), length.astype(jnp.int32)])

    resid = lax.dynamic_index_in_dim(inputs, section, 0, keepdims=False).astype(F32)
    residuals = []
    kept = []
    produced = []
    for layer in range(2):
        residuals.append(resid)
        result, saved = forward_layer(
            resid, weights[layer], gains[layer], layer == 0, tables[layer], scalars
        )
        kept.append(saved)
        produced.append(result.astype(BF16))
        resid = produced[-1].astype(F32)

    grad = lax.dynamic_index_in_dim(cotangent, section, 0, keepdims=False).astype(F32)
    sent_back = [None, None]
    attn_pieces = [None, None]
    mlp_pieces = [None, None]
    gain_grads = [None, None]
    for layer in (1, 0):
        d_resid, grad_attn, grad_mlp, gain_grads[layer] = backward_layer(
            grad,
            residuals[layer],
            kept[layer],
            weights[layer],
            gains[layer],
            layer == 0,
            tables[layer],
            scalars,
        )
        mlp_pieces[layer] = reduce_pack(grad_mlp)
        attn_pieces[layer] = reduce_pack(grad_attn)
        sent_back[layer] = d_resid.astype(BF16)
        grad = sent_back[layer].astype(F32)

    def by_layer(pair):
        mine = jnp.where(first, pair[0], pair[1])
        other = swap(jnp.where(first, pair[1], pair[0]))
        return jnp.stack([jnp.where(first, mine, other), jnp.where(first, other, mine)])[None]

    def whole(pair):
        mine = jnp.where(first, pair[0], pair[1])
        other = swap(jnp.where(first, pair[1], pair[0]))
        low = jnp.where(first, mine, other)
        high = jnp.where(first, other, mine)
        return jnp.concatenate([low, high], axis=1).astype(F32)[None]

    attn_grad = whole(attn_pieces)
    mlp_grad = whole(mlp_pieces)
    summed = lax.psum(jnp.concatenate(gain_grads, axis=0), ("section", "dp", "tensor"))
    shard = norm_gains.shape[1]
    gain_grad = lax.dynamic_slice(
        summed, (2 * section, lax.axis_index("dp") * shard), (2, shard)
    ).T[None]
    return (
        by_layer(produced),
        by_layer(sent_back),
        attn_grad[:, :, :head_width],
        attn_grad[:, :, head_width : 2 * head_width],
        attn_grad[:, :, 2 * head_width : 3 * head_width],
        attn_grad[:, :, 3 * head_width :],
        mlp_grad[:, :, :units],
        mlp_grad[:, :, units : 2 * units],
        mlp_grad[:, :, 2 * units :],
        gain_grad,
    )


def solution(mesh):
    rows = P(None, ("dp", "tensor"), None)
    weight = P("section", "dp", "tensor")
    gain = P("section", "dp", None)
    out_rows = P("section", None, ("dp", "tensor"), None)
    return jax.shard_map(
        local_program,
        mesh=mesh,
        in_specs=(rows, P(None, "dp"), rows) + (weight,) * 7 + (gain,),
        out_specs=(out_rows, out_rows) + (weight,) * 7 + (gain,),
        check_vma=False,
    )
```

time: 1650 us -> 500 us (0.30)
  waiting for transfers between devices: 913 us -> 176 us
  matrix products: 241 us -> 57 us
  local copies, waits for them, and re-layouts: 185 us -> 36.2 us
  blocking collectives: 136 us -> 38.9 us
  other arithmetic: 126 us -> 37.5 us
  Pallas kernels: 0 us -> 67.7 us
  starting transfers between devices: 9.48 us -> 61.8 us
    unnamed x72 -> x10, waiting for transfers between devices: 339 us -> 0.16 us
    reduce_scatter x12 -> x0, waiting for transfers between devices: 308 us -> none  [the longest x3 95.3 us: forward_layer(): lax.psum_scatter(branch.astype(jnp.bfloat16), 'tensor', scatter_dimension...]
    all_gather x12 -> x2, waiting for transfers between devices: 259 us -> 33.2 us  [the longest x1 33.2 us: local_program(): attn_all = lax.all_gather(attn_pack, ('section', 'dp'), axis=0, tiled=True)]
    dot_general x84 -> x24, matrix products: 241 us -> 57 us  [the longest x2 8.82 us: forward_layer(): qkv = jnp.dot(rows_one, w_qkv, preferred_element_type=F32)]
    unnamed x564 -> x179, local copies, waits for them, and re-layouts: 182 us -> 24.3 us
    ppermute x4 -> x52, waiting for transfers between devices: 7.41 us -> 143 us  [the longest x48 142 us: exchange(): return lax.ppermute(value, 'tensor', [(i, i ^ by) for i in range(count)])]
    all_gather x8 -> x0, blocking collectives: 125 us -> none  [the longest x1 17.1 us: fetch_weights(): lax.all_gather(params[5], 'dp', axis=1, tiled=True)]
    pallas_call x0 -> x4, Pallas kernels: none -> 67.7 us  [the longest x2 36.6 us: attend_back(): pl.pallas_call(functools.partial(attend_back_kernel, local=local, own=own...]
  transfers between devices with their start and end apart: 52 -> 58, of which waited for: 43 -> 29; matrix products, arithmetic and copies ran while one was open for 18% -> 20% of each run, Pallas kernels for 0% -> 10%
where the time goes in v1:
time: 500 us; the launch traced here: 491 us
  waiting for transfers between devices  176 us (35%)
  Pallas kernels  67.7 us (14%)
  starting transfers between devices  61.8 us (12%)
  matrix products  57 us (11%)
  blocking collectives  38.9 us (8%)
  other arithmetic  37.5 us (8%)
  local copies, waits for them, and re-layouts  36.2 us (7%)
  between operations  15.9 us (3%)
    ppermute x48, waiting for transfers between devices, exchange(): return lax.ppermute(value, 'tensor', [(i, i ^ by) for i in range(count)])  142 us
    ppermute x48, starting transfers between devices, exchange(): return lax.ppermute(value, 'tensor', [(i, i ^ by) for i in range(count)])  60.7 us
    psum x1, blocking collectives, local_program(): lax.psum(jnp.concatenate(gain_grads, axis=0), ('section', 'dp', 'tensor'))  38.9 us
    pallas_call x2, Pallas kernels, attend_back(): pl.pallas_call(functools.partial(attend_back_kernel, local=local, own=own...  36.6 us
    all_gather x1, waiting for transfers between devices, local_program(): attn_all = lax.all_gather(attn_pack, ('section', 'dp'), axis=0, tiled=True)  33.2 us
    pallas_call x2, Pallas kernels, attend(): pl.pallas_call(functools.partial(attend_kernel, local=local, own=own, dev...  31.2 us
    unnamed x179, local copies, waits for them, and re-layouts  24.3 us
  transfers between devices with their start and end apart: 58, of which 29 were waited for; matrix products, arithmetic and copies ran while one was open for 20% of the time, Pallas kernels for 10%

profile of v1, /device:TPU:0, one launch (start us, length us, event | category | flops | bytes accessed | tf_op | source)
XLA Modules:
  0.0 491.2 jit_solution(11598396353708779725)
XLA Ops:
  14.6 33.2 %all-gather.5.cloned.1.call-done = bf16[1,1536,770]{2,1,0:T(8,128)(2,1)} async-done(((bf16[1,192,770]{2,1,0:T(8,128)(2,1)}), bf16[1,1536,770]{2,1,0:T(8,128)(2,1)}) %all-gather.5.cloned.1.call-update) | async-done | bytes 2365456 | tf_op jit(solution)/shard_map/all_gather | solution.py:312
  61.6 8.9 %collective-permute-done.1 = bf16[256,768]{0,1:T(8,128)(2,1)S(1)} collective-permute-done((bf16[256,768]{0,1:T(8,128)(2,1)S(1)}, bf16[256,768]{0,1:T(8,128)(2,1)S(1)}, u32[]{:S(2)}, u32[]{:S(2)}) %collective-permute-start.1) | collective-permute-done | bytes 393248 | tf_op jit(solution)/shard_map/ppermute | solution.py:33
  70.4 4.4 fusion.42.qkv
  74.9 13.6 %attend.2 = (bf16[3,1024,64]{2,1,0:T(8,128)(2,1)}, bf16[3,1024,64]{2,1,0:T(8,128)(2,1)}, bf16[3,1024,64]{2,1,0:T(8,128)(2,1)}, bf16[1024,192]{1,0:T(8,128)(2,1)}, f32[3,8,1024]{2,1,0:T(8,128)}) custom-call(s32[2]{0:T(128)} %pad_add_fusion.scalars, f32[1024,576]{1,0:T(8,128)} %fusion.42.qkv, f32[1024,64]{1,0:T(8,128)} %get-tuple-element.156.cosine, ...), custom_call_target="tpu_custom_call" | custom-call | tf_op jit(solution)/shard_map/attend/pallas_call | solution.py:148
  94.0 8.5 %collective-permute-done.3 = bf16[256,768]{0,1:T(8,128)(2,1)S(1)} collective-permute-done((bf16[256,768]{0,1:T(8,128)(2,1)S(1)}, bf16[256,768]{0,1:T(8,128)(2,1)S(1)}, u32[]{:S(2)}, u32[]{:S(2)}) %collective-permute-start.3) | collective-permute-done | bytes 393248 | tf_op jit(solution)/shard_map/ppermute | solution.py:33
  102.5 7.7 %collective-permute-done.4 = bf16[256,768]{0,1:T(8,128)(2,1)S(1)} collective-permute-done((bf16[256,768]{0,1:T(8,128)(2,1)S(1)}, bf16[256,768]{0,1:T(8,128)(2,1)S(1)}, u32[]{:S(2)}, u32[]{:S(2)}) %collective-permute-start.4) | collective-permute-done | bytes 393248 | tf_op jit(solution)/shard_map/ppermute | solution.py:33
  115.0 8.5 %collective-permute-done.6 = bf16[256,768]{0,1:T(8,128)(2,1)S(1)} collective-permute-done((bf16[256,768]{0,1:T(8,128)(2,1)S(1)}, bf16[256,768]{0,1:T(8,128)(2,1)S(1)}, u32[]{:S(2)}, u32[]{:S(2)}) %collective-permute-start.6) | collective-permute-done | bytes 393248 | tf_op jit(solution)/shard_map/ppermute | solution.py:33
  123.5 5.9 %collective-permute-done.7 = bf16[256,768]{0,1:T(8,128)(2,1)} collective-permute-done((bf16[256,768]{0,1:T(8,128)(2,1)S(1)}, bf16[256,768]{0,1:T(8,128)(2,1)}, u32[]{:S(2)}, u32[]{:S(2)}) %collective-permute-start.7) | collective-permute-done | bytes 393248 | tf_op jit(solution)/shard_map/ppermute | solution.py:33
  141.9 12.6 %collective-permute-done.10 = bf16[256,768]{0,1:T(8,128)(2,1)S(1)} collective-permute-done((bf16[256,768]{0,1:T(8,128)(2,1)S(1)}, bf16[256,768]{0,1:T(8,128)(2,1)S(1)}, u32[]{:S(2)}, u32[]{:S(2)}) %collective-permute-start.10) | collective-permute-done | bytes 393248 | tf_op jit(solution)/shard_map/ppermute | solution.py:33
  161.4 7.2 %collective-permute-done.12 = bf16[256,768]{0,1:T(8,128)(2,1)S(1)} collective-permute-done((bf16[256,768]{0,1:T(8,128)(2,1)S(1)}, bf16[256,768]{0,1:T(8,128)(2,1)S(1)}, u32[]{:S(2)}, u32[]{:S(2)}) %collective-permute-start.12) | collective-permute-done | bytes 393248 | tf_op jit(solution)/shard_map/ppermute | solution.py:33
  168.5 6.7 %collective-permute-done.13 = bf16[256,768]{0,1:T(8,128)(2,1)S(1)} collective-permute-done((bf16[256,768]{0,1:T(8,128)(2,1)S(1)}, bf16[256,768]{0,1:T(8,128)(2,1)S(1)}, u32[]{:S(2)}, u32[]{:S(2)}) %collective-permute-start.13) | collective-permute-done | bytes 393248 | tf_op jit(solution)/shard_map/ppermute | solution.py:33
  175.3 4.4 fusion.36.qkv
  179.7 17.6 %attend.3 = (bf16[3,1024,64]{2,1,0:T(8,128)(2,1)}, bf16[3,1024,64]{2,1,0:T(8,128)(2,1)}, bf16[3,1024,64]{2,1,0:T(8,128)(2,1)}, bf16[1024,192]{1,0:T(8,128)(2,1)}, f32[3,8,1024]{2,1,0:T(8,128)}) custom-call(s32[2]{0:T(128)} %pad_add_fusion.scalars, f32[1024,576]{1,0:T(8,128)} %fusion.36.qkv, f32[1024,64]{1,0:T(8,128)} %get-tuple-element.158.cosine, ...), custom_call_target="tpu_custom_call" | custom-call | tf_op jit(solution)/shard_map/attend/pallas_call | solution.py:148
  202.8 8.2 %collective-permute-done.15 = bf16[256,768]{0,1:T(8,128)(2,1)S(1)} collective-permute-done((bf16[256,768]{0,1:T(8,128)(2,1)S(1)}, bf16[256,768]{0,1:T(8,128)(2,1)S(1)}, u32[]{:S(2)}, u32[]{:S(2)}) %collective-permute-start.15) | collective-permute-done | bytes 393248 | tf_op jit(solution)/shard_map/ppermute | solution.py:33
  223.0 6.3 %collective-permute-done.18 = bf16[256,768]{0,1:T(8,128)(2,1)} collective-permute-done((bf16[256,768]{0,1:T(8,128)(2,1)S(1)}, bf16[256,768]{0,1:T(8,128)(2,1)}, u32[]{:S(2)}, u32[]{:S(2)}) %collective-permute-start.18) | collective-permute-done | bytes 393248 | tf_op jit(solution)/shard_map/ppermute | solution.py:33
  230.3 8.9 %collective-permute-done.19 = bf16[256,768]{0,1:T(8,128)(2,1)} collective-permute-done((bf16[256,768]{0,1:T(8,128)(2,1)S(1)}, bf16[256,768]{0,1:T(8,128)(2,1)}, u32[]{:S(2)}, u32[]{:S(2)}) %collective-permute-start.19) | collective-permute-done | bytes 393248 | tf_op jit(solution)/shard_map/ppermute | solution.py:33
  265.9 5.7 %collective-permute-done.29 = bf16[256,768]{0,1:T(8,128)(2,1)S(1)} collective-permute-done((bf16[256,768]{0,1:T(8,128)(2,1)S(1)}, bf16[256,768]{0,1:T(8,128)(2,1)S(1)}, u32[]{:S(2)}, u32[]{:S(2)}) %collective-permute-start.29) | collective-permute-done | bytes 393248 | tf_op jit(solution)/shard_map/ppermute | solution.py:33
  295.5 21.8 %attend_back.2 = bf16[1024,576]{1,0:T(8,128)(2,1)} custom-call(s32[2]{0:T(128)} %pad_add_fusion.scalars, bf16[3,1024,64]{2,1,0:T(8,128)(2,1)} %get-tuple-element.25.q3, bf16[3,1024,64]{2,1,0:T(8,128)(2,1)} %get-tuple-element.26.k3, bf16[3,1024,64]{2,1,0:T(8,128)(2,1)} %get-tuple-element.27.v3, bf16[1024,192]{1,0:T(8,128)(2,1)} %copy.92.grad, ...), custom_call_target="tpu_custom_call" | custom-call | tf_op jit(solution)/shard_map/attend_back/pallas_call | solution.py:228
  331.0 4.4 collective-permute-done.36
  349.5 4.6 collective-permute-done.38
  370.8 5.0 %collective-permute-done.41 = bf16[256,768]{0,1:T(8,128)(2,1)S(1)} collective-permute-done((bf16[256,768]{0,1:T(8,128)(2,1)}, bf16[256,768]{0,1:T(8,128)(2,1)S(1)}, u32[]{:S(2)}, u32[]{:S(2)}) %collective-permute-start.41) | collective-permute-done | bytes 393248 | tf_op jit(solution)/shard_map/ppermute | solution.py:33
  387.7 5.9 %collective-permute-done.44 = bf16[256,768]{0,1:T(8,128)(2,1)} collective-permute-done((bf16[256,768]{0,1:T(8,128)(2,1)S(1)}, bf16[256,768]{0,1:T(8,128)(2,1)}, u32[]{:S(2)}, u32[]{:S(2)}) %collective-permute-start.44) | collective-permute-done | bytes 393248 | tf_op jit(solution)/shard_map/ppermute | solution.py:33
  396.6 14.7 %attend_back.3 = bf16[1024,576]{1,0:T(8,128)(2,1)} custom-call(s32[2]{0:T(128)} %pad_add_fusion.scalars, bf16[3,1024,64]{2,1,0:T(8,128)(2,1)} %get-tuple-element.22.q3, bf16[3,1024,64]{2,1,0:T(8,128)(2,1)} %get-tuple-element.23.k3, bf16[3,1024,64]{2,1,0:T(8,128)(2,1)} %get-tuple-element.24.v3, bf16[1024,192]{1,0:T(8,128)(2,1)} %copy.95.grad, ...), custom_call_target="tpu_custom_call" | custom-call | tf_op jit(solution)/shard_map/attend_back/pallas_call | solution.py:228
  432.0 38.9 %psum.7 = f32[4,768]{1,0:T(4,128)S(1)} all-reduce(f32[4,768]{1,0:T(4,128)S(1)} %pad_maximum_fusion.39), channel_id=1, replica_groups=mesh['section'=2,'dp'=4,'tensor'=4] {'section','dp','tensor'}, use_global_device_ids=true, to_apply=%region_24.25 | all-reduce | flops 3072 | bytes 24576 | tf_op jit(solution)/shard_map/psum | solution.py:382
  (404 shorter events, 211.5 us)
Async XLA Ops:
  7.2 40.6 %all-gather.5.cloned.1.call-start = ((), (), s32[]{:S(2)}) async-start(), calls=%async_computation.4 | async-start | bytes 3096576 | tf_op jit(solution)/shard_map/all_gather | solution.py:312
  10.1 104.9 %all-gather.7.cloned.1.call-start = ((), (), s32[]{:S(2)}) async-start(), calls=%async_computation.5 | async-start | bytes 3096576 | tf_op jit(solution)/shard_map/all_gather | solution.py:313
  12.1 413.7 %reduce-scatter.19.cloned.1.call-start = ((), (), s32[]{:S(2)}) async-start(), calls=%async_computation.9 | async-start | bytes 1769472
  51.0 19.4 %collective-permute-start.1 = (bf16[256,768]{0,1:T(8,128)(2,1)S(1)}, bf16[256,768]{0,1:T(8,128)(2,1)S(1)}, u32[]{:S(2)}, u32[]{:S(2)}) collective-permute-start(bf16[256,768]{0,1:T(8,128)(2,1)S(1)} %fusion.46), channel_id=1, source_target_pairs={{0,2},{1,3},{2,0},{3,1},{4,6},{5,7},{6,4},{7,5},{8,10},{9,11},{10,... | collective-permute-start | bytes 1179656 | tf_op jit(solution)/shard_map/ppermute | solution.py:33
  52.5 17.9 %collective-permute-start.2 = (bf16[256,768]{0,1:T(8,128)(2,1)S(1)}, bf16[256,768]{0,1:T(8,128)(2,1)S(1)}, u32[]{:S(2)}, u32[]{:S(2)}) collective-permute-start(bf16[256,768]{0,1:T(8,128)(2,1)S(1)} %fusion.46), channel_id=1, source_target_pairs={{0,3},{1,2},{2,1},{3,0},{4,7},{5,6},{6,5},{7,4},{8,11},{9,10},{10,... | collective-permute-start | bytes 1179656 | tf_op jit(solution)/shard_map/ppermute | solution.py:33
  91.5 18.6 %collective-permute-start.4 = (bf16[256,768]{0,1:T(8,128)(2,1)S(1)}, bf16[256,768]{0,1:T(8,128)(2,1)S(1)}, u32[]{:S(2)}, u32[]{:S(2)}) collective-permute-start(bf16[256,768]{0,1:T(8,128)(2,1)S(1)} %get-tuple-element.133), channel_id=1, source_target_pairs={{0,2},{1,3},{2,0},{3,1},{4,6},{5,7},{6,4},{7,5},{8,10},{9,11},{10,... | collective-permute-start | bytes 1179656 | tf_op jit(solution)/shard_map/ppermute | solution.py:33
  92.5 17.6 %collective-permute-start.5 = (bf16[256,768]{0,1:T(8,128)(2,1)S(1)}, bf16[256,768]{0,1:T(8,128)(2,1)S(1)}, u32[]{:S(2)}, u32[]{:S(2)}) collective-permute-start(bf16[256,768]{0,1:T(8,128)(2,1)S(1)} %get-tuple-element.132), channel_id=1, source_target_pairs={{0,3},{1,2},{2,1},{3,0},{4,7},{5,6},{6,5},{7,4},{8,11},{9,10},{10,... | collective-permute-start | bytes 1179656 | tf_op jit(solution)/shard_map/ppermute | solution.py:33
  112.1 17.3 %collective-permute-start.7 = (bf16[256,768]{0,1:T(8,128)(2,1)S(1)}, bf16[256,768]{0,1:T(8,128)(2,1)}, u32[]{:S(2)}, u32[]{:S(2)}) collective-permute-start(bf16[256,768]{0,1:T(8,128)(2,1)S(1)} %multiply_convert_fusion.5), channel_id=1, source_target_pairs={{0,2},{1,3},{2,0},{3,1},{4,6},{5,7},{6,4},{7,5},{8,10},{9,11},{10,... | collective-permute-start | bytes 1179656 | tf_op jit(solution)/shard_map/ppermute | solution.py:33
  158.3 17.0 %collective-permute-start.13 = (bf16[256,768]{0,1:T(8,128)(2,1)S(1)}, bf16[256,768]{0,1:T(8,128)(2,1)S(1)}, u32[]{:S(2)}, u32[]{:S(2)}) collective-permute-start(bf16[256,768]{0,1:T(8,128)(2,1)S(1)} %fusion.44), channel_id=1, source_target_pairs={{0,2},{1,3},{2,0},{3,1},{4,6},{5,7},{6,4},{7,5},{8,10},{9,11},{10,... | collective-permute-start | bytes 1179656 | tf_op jit(solution)/shard_map/ppermute | solution.py:33
  158.6 16.6 %collective-permute-start.14 = (bf16[256,768]{0,1:T(8,128)(2,1)S(1)}, bf16[256,768]{0,1:T(8,128)(2,1)S(1)}, u32[]{:S(2)}, u32[]{:S(2)}) collective-permute-start(bf16[256,768]{0,1:T(8,128)(2,1)S(1)} %fusion.44), channel_id=1, source_target_pairs={{0,3},{1,2},{2,1},{3,0},{4,7},{5,6},{6,5},{7,4},{8,11},{9,10},{10,... | collective-permute-start | bytes 1179656 | tf_op jit(solution)/shard_map/ppermute | solution.py:33
  219.2 20.0 %collective-permute-start.19 = (bf16[256,768]{0,1:T(8,128)(2,1)S(1)}, bf16[256,768]{0,1:T(8,128)(2,1)}, u32[]{:S(2)}, u32[]{:S(2)}) collective-permute-start(bf16[256,768]{0,1:T(8,128)(2,1)S(1)} %multiply_convert_fusion.4), channel_id=1, source_target_pairs={{0,2},{1,3},{2,0},{3,1},{4,6},{5,7},{6,4},{7,5},{8,10},{9,11},{10,... | collective-permute-start | bytes 1179656 | tf_op jit(solution)/shard_map/ppermute | solution.py:33
  219.2 20.0 %collective-permute-start.20 = (bf16[256,768]{0,1:T(8,128)(2,1)S(1)}, bf16[256,768]{0,1:T(8,128)(2,1)}, u32[]{:S(2)}, u32[]{:S(2)}) collective-permute-start(bf16[256,768]{0,1:T(8,128)(2,1)S(1)} %multiply_convert_fusion.4), channel_id=1, source_target_pairs={{0,3},{1,2},{2,1},{3,0},{4,7},{5,6},{6,5},{7,4},{8,11},{9,10},{10,... | collective-permute-start | bytes 1179656 | tf_op jit(solution)/shard_map/ppermute | solution.py:33
  221.0 23.8 %collective-permute-start.25 = (bf16[256,768]{0,1:T(8,128)(2,1)S(1)}, bf16[256,768]{0,1:T(8,128)(2,1)S(1)}, u32[]{:S(2)}, u32[]{:S(2)}) collective-permute-start(bf16[256,768]{0,1:T(8,128)(2,1)S(1)} %bitcast.85), channel_id=1, source_target_pairs={{0,1},{1,0},{2,3},{3,2},{4,5},{5,4},{6,7},{7,6},{8,9},{9,8},{10,11... | collective-permute-start | bytes 1179656 | tf_op jit(solution)/shard_map/ppermute | solution.py:33
  223.0 26.2 %collective-permute-start.26 = (bf16[256,768]{0,1:T(8,128)(2,1)S(1)}, bf16[256,768]{0,1:T(8,128)(2,1)}, u32[]{:S(2)}, u32[]{:S(2)}) collective-permute-start(bf16[256,768]{0,1:T(8,128)(2,1)S(1)} %bitcast.86), channel_id=1, source_target_pairs={{0,2},{1,3},{2,0},{3,1},{4,6},{5,7},{6,4},{7,5},{8,10},{9,11},{10,... | collective-permute-start | bytes 1179656 | tf_op jit(solution)/shard_map/ppermute | solution.py:33
  229.2 19.9 %collective-permute-start.27 = (bf16[256,768]{0,1:T(8,128)(2,1)S(1)}, bf16[256,768]{0,1:T(8,128)(2,1)}, u32[]{:S(2)}, u32[]{:S(2)}) collective-permute-start(bf16[256,768]{0,1:T(8,128)(2,1)S(1)} %bitcast.87), channel_id=1, source_target_pairs={{0,3},{1,2},{2,1},{3,0},{4,7},{5,6},{6,5},{7,4},{8,11},{9,10},{10,... | collective-permute-start | bytes 1179656 | tf_op jit(solution)/shard_map/ppermute | solution.py:33
  274.5 17.7 %collective-permute-start.32 = (bf16[256,768]{0,1:T(8,128)(2,1)}, bf16[256,768]{0,1:T(8,128)(2,1)}, u32[]{:S(2)}, u32[]{:S(2)}) collective-permute-start(bf16[256,768]{0,1:T(8,128)(2,1)} %fusion.58), channel_id=1, source_target_pairs={{0,2},{1,3},{2,0},{3,1},{4,6},{5,7},{6,4},{7,5},{8,10},{9,11},{10,... | collective-permute-start | bytes 1179656 | tf_op jit(solution)/shard_map/ppermute | solution.py:33
  281.6 189.9 %reduce-scatter.15.cloned.1.call-start = ((), (), s32[]{:S(2)}) async-start(), calls=%async_computation.7 | async-start | bytes 1327104
  284.1 56.3 %collective-permute-start.21 = (bf16[256,768]{0,1:T(8,128)(2,1)}, bf16[256,768]{0,1:T(8,128)(2,1)}, u32[]{:S(2)}, u32[]{:S(2)}) collective-permute-start(bf16[256,768]{0,1:T(8,128)(2,1)} %get-tuple-element.122), channel_id=1, source_target_pairs={{0,1},{1,0},{2,3},{3,2},{4,5},{5,4},{6,7},{7,6},{8,9},{9,8},{10,11... | collective-permute-start | bytes 1179656 | tf_op jit(solution)/shard_map/ppermute | solution.py:33
  285.6 60.2 %collective-permute-start.22 = (bf16[256,768]{0,1:T(8,128)(2,1)}, bf16[256,768]{0,1:T(8,128)(2,1)}, u32[]{:S(2)}, u32[]{:S(2)}) collective-permute-start(bf16[256,768]{0,1:T(8,128)(2,1)} %get-tuple-element.124), channel_id=1, source_target_pairs={{0,2},{1,3},{2,0},{3,1},{4,6},{5,7},{6,4},{7,5},{8,10},{9,11},{10,... | collective-permute-start | bytes 1179656 | tf_op jit(solution)/shard_map/ppermute | solution.py:33
  328.4 17.4 %collective-permute-start.23 = (bf16[256,768]{0,1:T(8,128)(2,1)}, bf16[256,768]{0,1:T(8,128)(2,1)}, u32[]{:S(2)}, u32[]{:S(2)}) collective-permute-start(bf16[256,768]{0,1:T(8,128)(2,1)} %get-tuple-element.123), channel_id=1, source_target_pairs={{0,3},{1,2},{2,1},{3,0},{4,7},{5,6},{6,5},{7,4},{8,11},{9,10},{10,... | collective-permute-start | bytes 1179656 | tf_op jit(solution)/shard_map/ppermute | solution.py:33
  345.5 127.1 %reduce-scatter.17.cloned.1.call-start = ((), (), s32[]{:S(2)}) async-start(), calls=%async_computation.8 | async-start | bytes 1769472
  348.5 34.7 %collective-permute-start.24 = (bf16[256,768]{0,1:T(8,128)(2,1)}, bf16[256,768]{0,1:T(8,128)(2,1)}, u32[]{:S(2)}, u32[]{:S(2)}) collective-permute-start(bf16[256,768]{0,1:T(8,128)(2,1)} %get-tuple-element.94), channel_id=1, source_target_pairs={{0,16},{16,0},{1,17},{17,1},{2,18},{18,2},{3,19},{19,3},{4,20},{20... | collective-permute-start | bytes 1179656 | tf_op jit(solution)/shard_map/ppermute | solution.py:370
  370.7 105.8 %reduce-scatter.13.cloned.1.call-start = ((), (), s32[]{:S(2)}) async-start(), calls=%async_computation.6 | async-start | bytes 1327104
  431.7 42.2 %collective-permute-start.49 = (bf16[256,768]{0,1:T(8,128)(2,1)S(1)}, bf16[256,768]{0,1:T(8,128)(2,1)S(1)}, u32[]{:S(2)}, u32[]{:S(2)}) collective-permute-start(bf16[256,768]{0,1:T(8,128)(2,1)S(1)} %get-tuple-element.82), channel_id=1, source_target_pairs={{0,16},{16,0},{1,17},{17,1},{2,18},{18,2},{3,19},{19,3},{4,20},{20... | collective-permute-start | bytes 1179656 | tf_op jit(solution)/shard_map/ppermute | solution.py:370
  (116 other events, 1119.9 us)
Sparse Core Ops, SparseCore 0:
  10.2 37.5 all-gather.4
  50.0 33.9 all-gather.6
  281.8 38.7 reduce-scatter.18
  345.6 34.9 reduce-scatter.14
  382.7 38.5 reduce-scatter.16
  425.9 34.8 reduce-scatter.12

commit v2 on v1

--- a/solution.py
+++ b/solution.py
@@ -34,17 +34,60 @@
 
 
 def gather_rows(rows):
-    count = lax.axis_size("tensor")
-    return jnp.concatenate([rows] + [exchange(rows, by) for by in range(1, count)], axis=0)
-
-
-def scatter_rows(partial):
-    count = lax.axis_size("tensor")
-    own = partial.shape[0] // count
-    total = partial[:own].astype(F32)
-    for by in range(1, count):
-        total = total + exchange(partial[by * own : (by + 1) * own], by).astype(F32)
+    return [rows] + [exchange(rows, by) for by in range(1, lax.axis_size("tensor"))]
+
+
+def scatter_rows(blocks):
+    moved = [exchange(block, by) for by, block in enumerate(blocks) if by]
+    total = blocks[0].astype(F32)
+    for block in moved:
+        total = total + block.astype(F32)
     return total
+
+
+def over(value, axis, by):
+    count = lax.axis_size(axis)
+    return lax.ppermute(value, axis, [(i, i ^ by) for i in range(count)])
+
+
+def butterfly(value, axes):
+    for axis in axes:
+        by = 1
+        while by < lax.axis_size(axis):
+            value = value + over(value, axis, by)
+            by *= 2
+    return value
+
+
+def dp_gather(shard):
+    count = lax.axis_size("dp")
+    if count > 8:
+        return lax.all_gather(shard, "dp", axis=0, tiled=True)
+    rows = shard.shape[0]
+    index = lax.axis_index("dp")
+    full = jnp.zeros((count * rows,) + shard.shape[1:], shard.dtype)
+    for by in range(count):
+        block = over(shard, "dp", by) if by else shard
+        full = lax.dynamic_update_slice_in_dim(full, block, (index ^ by) * rows, 0)
+    return full
+
+
+def dp_scatter(full):
+    count = lax.axis_size("dp")
+    if count > 8:
+        return lax.psum_scatter(full, "dp", scatter_dimension=0, tiled=True)
+    rows = full.shape[0] // count
+    index = lax.axis_index("dp")
+    total = None
+    for by in range(count):
+        block = lax.dynamic_slice_in_dim(full, (index ^ by) * rows, rows, 0)
+        block = (over(block, "dp", by) if by else block).astype(F32)
+        total = block if total is None else total + block
+    return total.astype(full.dtype)
+
+
+def swap(value):
+    return over(value, "section", 1)
 
 
 def positions(own, devices):
@@ -78,16 +121,21 @@
     return place, pl.multiple_of(before, HALF_WINDOW), pl.multiple_of(after, HALF_WINDOW)
 
 
-def attend_kernel(scalars, qkv, cosine, sine, q3, k3, v3, out, lse, *, local, own, devices, heads):
+def attend_kernel(scalars, cosine, sine, *refs, local, own, devices, heads):
+    blocks = refs[:devices]
+    q3, k3, v3, out, lse = refs[devices:]
     count = own * devices
     width = heads * HEAD
     length = scalars[1]
     for head in range(heads):
         at = head * HEAD
-        for part, store in ((0, q3), (1, k3)):
-            rows = qkv[:, part * width + at : part * width + at + HEAD]
-            store[head] = (rows * cosine[...] + turn(rows) * sine[...]).astype(BF16)
-        v3[head] = qkv[:, 2 * width + at : 2 * width + at + HEAD].astype(BF16)
+        for index, qkv in enumerate(blocks):
+            here = slice(index * own, (index + 1) * own)
+            for part, store in ((0, q3), (1, k3)):
+                rows = qkv[:, part * width + at : part * width + at + HEAD]
+                turned = rows * cosine[here, :] + turn(rows) * sine[here, :]
+                store[head, here, :] = turned.astype(BF16)
+            v3[head, here, :] = qkv[:, 2 * width + at : 2 * width + at + HEAD].astype(BF16)
     for head in range(heads):
 
         def step(block, carry):
@@ -154,15 +202,19 @@
             jax.ShapeDtypeStruct((count, heads * HEAD), BF16),
             jax.ShapeDtypeStruct((heads, 8, count), F32),
         ),
-        in_specs=[pl.BlockSpec(memory_space=pltpu.SMEM), vmem, vmem, vmem],
+        in_specs=[pl.BlockSpec(memory_space=pltpu.SMEM)] + [vmem] * (2 + devices),
         out_specs=(vmem, vmem, vmem, vmem, vmem),
         name="attend",
-    )(scalars, qkv, cosine, sine)
+    )(scalars, cosine, sine, *qkv)
 
 
 def attend_back_kernel(
-    scalars, q3, k3, v3, grad, lse, cosine, sine, out, dk, dv, *, local, own, devices, heads
+    scalars, q3, k3, v3, lse, cosine, sine, *refs, local, own, devices, heads
 ):
+    blocks = refs[:devices]
+    out, dk, dv, grad = refs[devices:]
+    for index, block in enumerate(blocks):
+        grad[index * own : (index + 1) * own, :] = block[...]
     count = own * devices
     width = heads * HEAD
     length = scalars[1]
@@ -228,62 +280,83 @@
     return pl.pallas_call(
         functools.partial(attend_back_kernel, local=local, own=own, devices=devices, heads=heads),
         out_shape=jax.ShapeDtypeStruct((count, 3 * heads * HEAD), BF16),
-        in_specs=[pl.BlockSpec(memory_space=pltpu.SMEM)] + [vmem] * 7,
+        in_specs=[pl.BlockSpec(memory_space=pltpu.SMEM)] + [vmem] * (6 + devices),
         out_specs=vmem,
-        scratch_shapes=[pltpu.VMEM((count, HEAD), F32), pltpu.VMEM((count, HEAD), F32)],
+        scratch_shapes=[
+            pltpu.VMEM((count, HEAD), F32),
+            pltpu.VMEM((count, HEAD), F32),
+            pltpu.VMEM((count, heads * HEAD), BF16),
+        ],
         name="attend_back",
-    )(scalars, q3, k3, v3, grad, lse, cosine, sine)
+    )(scalars, q3, k3, v3, lse, cosine, sine, *grad)
+
+
+def cut(rows, own):
+    return [rows[at : at + own] for at in range(0, rows.shape[0], own)]
+
+
+def product(blocks, weight):
+    return [jnp.dot(block, weight, preferred_element_type=F32) for block in blocks]
+
+
+def product_back(blocks, weight):
+    return [lax.dot_general(block, weight, NT, preferred_element_type=F32) for block in blocks]
+
+
+def low(blocks):
+    return [block.astype(BF16) for block in blocks]
 
 
 def forward_layer(resid, weights, gains, local, tables, scalars):
     w_qkv, w_out, w_in, w_down = weights
     own = resid.shape[0]
     devices = lax.axis_size("tensor")
-    heads = w_out.shape[1] // HEAD
+    heads = w_out().shape[1] // HEAD
     rows_one = gather_rows(layer_norm(resid, gains[0]).astype(BF16))
-    qkv = jnp.dot(rows_one, w_qkv, preferred_element_type=F32)
+    qkv = product(rows_one, w_qkv())
     q3, k3, v3, attended, lse = attend(qkv, *tables, scalars, local, own, devices, heads)
-    branch = lax.dot_general(attended, w_out, NT, preferred_element_type=F32)
-    mixed = resid + scatter_rows(branch.astype(BF16))
+    branch = low(product_back(cut(attended, own), w_out()))
+    mixed = resid + scatter_rows(branch)
     rows_two = gather_rows(layer_norm(mixed, gains[1]).astype(BF16))
-    both = jnp.dot(rows_two, w_in, preferred_element_type=F32)
-    units = w_down.shape[1]
-    hidden = geglu(both[:, :units], both[:, units:]).astype(BF16)
-    down = lax.dot_general(hidden, w_down, NT, preferred_element_type=F32)
-    result = mixed + scatter_rows(down.astype(BF16))
+    both = product(rows_two, w_in())
+    units = w_down().shape[1]
+    hidden = [geglu(block[:, :units], block[:, units:]).astype(BF16) for block in both]
+    result = mixed + scatter_rows(low(product_back(hidden, w_down())))
     return result, (rows_one, q3, k3, v3, lse, attended, mixed, rows_two, both, hidden)
 
 
 def backward_layer(grad_out, resid, kept, weights, gains, local, tables, scalars):
-    w_qkv, w_out, w_in, w_down = weights
+    w_qkv, w_out, w_in, w_down = [weight() for weight in weights]
     rows_one, q3, k3, v3, lse, attended, mixed, rows_two, both, hidden = kept
     own = resid.shape[0]
     devices = lax.axis_size("tensor")
     heads = w_out.shape[1] // HEAD
     units = w_down.shape[1]
-    outer = functools.partial(jnp.einsum, "sd,sf->df", preferred_element_type=F32)
+
+    def outer(left, right):
+        left, right = [
+            jnp.concatenate(side, axis=0) if isinstance(side, list) else side
+            for side in (left, right)
+        ]
+        return jnp.einsum("sd,sf->df", left, right, preferred_element_type=F32).astype(BF16)
+
     grad_rows = gather_rows(grad_out.astype(BF16))
-    d_hidden = jnp.dot(grad_rows, w_down, preferred_element_type=F32)
-    _, pull_geglu = jax.vjp(geglu, both[:, :units], both[:, units:])
-    d_both = jnp.concatenate([part.astype(BF16) for part in pull_geglu(d_hidden)], axis=1)
-    d_two = lax.dot_general(d_both, w_in, NT, preferred_element_type=F32)
-    d_two = scatter_rows(d_two.astype(BF16))
-    grad_mlp = jnp.concatenate(
-        [outer(rows_two, d_both).astype(BF16), outer(grad_rows, hidden).astype(BF16)], axis=1
-    )
+    d_both = []
+    for block, d_hidden in zip(both, product(grad_rows, w_down)):
+        _, pull_geglu = jax.vjp(geglu, block[:, :units], block[:, units:])
+        d_both.append(jnp.concatenate(low(pull_geglu(d_hidden)), axis=1))
+    d_two = scatter_rows(low(product_back(d_both, w_in)))
+    grad_mlp = jnp.concatenate([outer(rows_two, d_both), outer(grad_rows, hidden)], axis=1)
     _, pull_second = jax.vjp(layer_norm, mixed, gains[1])
     d_mixed, gain_two = pull_second(d_two)
     d_mixed = d_mixed + grad_out
     mixed_rows = gather_rows(d_mixed.astype(BF16))
-    d_attended = jnp.dot(mixed_rows, w_out, preferred_element_type=F32).astype(BF16)
+    d_attended = low(product(mixed_rows, w_out))
     d_qkv = attend_back(
         q3, k3, v3, d_attended, lse, *tables, scalars, local, own, devices, heads
     )
-    d_one = lax.dot_general(d_qkv, w_qkv, NT, preferred_element_type=F32)
-    d_one = scatter_rows(d_one.astype(BF16))
-    grad_attn = jnp.concatenate(
-        [outer(rows_one, d_qkv).astype(BF16), outer(mixed_rows, attended).astype(BF16)], axis=1
-    )
+    d_one = scatter_rows(low(product_back(cut(d_qkv, own), w_qkv)))
+    grad_attn = jnp.concatenate([outer(rows_one, d_qkv), outer(mixed_rows, attended)], axis=1)
     _, pull_first = jax.vjp(layer_norm, resid, gains[0])
     d_resid, gain_one = pull_first(d_one)
     return d_resid + d_mixed, grad_attn, grad_mlp, jnp.stack([gain_one, gain_two])
@@ -293,6 +366,14 @@
     half = pack.shape[1] // 2
     halves = jnp.concatenate([pack[:, :half], pack[:, half:]], axis=0)
     return lax.psum_scatter(halves, ("section", "dp"), scatter_dimension=0, tiled=True)
+
+
+def reduce_last(pack):
+    half = pack.shape[1] // 2
+    first = lax.axis_index("section") == 0
+    mine = jnp.where(first, pack[:, :half], pack[:, half:])
+    other = swap(jnp.where(first, pack[:, half:], pack[:, :half]))
+    return dp_scatter((mine.astype(F32) + other.astype(F32)).astype(BF16))
 
 
 def local_program(
@@ -305,26 +386,45 @@
     features = inputs.shape[2]
     head_width = w_query.shape[2]
     units = w_gate.shape[2]
-    swap = functools.partial(lax.ppermute, axis_name="section", perm=[(0, 1), (1, 0)])
-
-    attn_pack = jnp.concatenate([w_query, w_key, w_value, w_out, norm_gains], axis=2)[0]
+
+    shard = norm_gains.shape[1]
+    spread = lax.dynamic_update_slice(
+        jnp.zeros((4, features), F32),
+        norm_gains[0].astype(F32).T,
+        (2 * section, lax.axis_index("dp") * shard),
+    )
+    all_gains = butterfly(spread, ("section", "dp"))
+    gains = [all_gains[:2], all_gains[2:]]
+
+    attn_shard = jnp.concatenate([w_query, w_key, w_value, w_out], axis=2)[0]
+    half = 2 * head_width
+    own_half = jnp.where(first, attn_shard[:, :half], attn_shard[:, half:])
+    got_half = swap(jnp.where(first, attn_shard[:, half:], attn_shard[:, :half]))
+    mine = dp_gather(jnp.where(first, own_half, got_half))
+    other = swap(mine)
+    low_half = jnp.where(first, mine, other)
+    high_half = jnp.where(first, other, mine)
+
     mlp_pack = jnp.concatenate([w_gate, w_up, w_down], axis=2)[0]
-    attn_all = lax.all_gather(attn_pack, ("section", "dp"), axis=0, tiled=True)
+    second, mlp_pack, _ = lax.optimization_barrier(
+        (jnp.where(first, got_half, own_half), mlp_pack, other)
+    )
     mlp_all = lax.all_gather(mlp_pack, ("section", "dp"), axis=0, tiled=True)
+    second = lax.all_gather(second, ("section", "dp"), axis=0, tiled=True)
+    halves = [(low_half, high_half), (second[:features], second[features:])]
     weights = []
-    gains = []
     for layer in range(2):
-        attn = attn_all[layer * features : (layer + 1) * features]
+        low_part, high_part = halves[layer]
         mlp = mlp_all[layer * features : (layer + 1) * features]
+        qkv = jnp.concatenate([low_part, high_part[:, :head_width]], axis=1)
         weights.append(
             (
-                attn[:, : 3 * head_width],
-                attn[:, 3 * head_width : 4 * head_width],
-                mlp[:, : 2 * units],
-                mlp[:, 2 * units :],
+                lambda qkv=qkv: qkv,
+                lambda high_part=high_part: high_part[:, head_width:],
+                lambda mlp=mlp: mlp[:, : 2 * units],
+                lambda mlp=mlp: mlp[:, 2 * units :],
             )
         )
-        gains.append(attn[:, 4 * head_width :].astype(F32).T)
 
     position = positions(own, devices)
     tables = [rotary_tables(position, theta) for theta in THETAS]
@@ -361,7 +461,7 @@
             scalars,
         )
         mlp_pieces[layer] = reduce_pack(grad_mlp)
-        attn_pieces[layer] = reduce_pack(grad_attn)
+        attn_pieces[layer] = reduce_pack(grad_attn) if layer else reduce_last(grad_attn)
         sent_back[layer] = d_resid.astype(BF16)
         grad = sent_back[layer].astype(F32)
 
@@ -379,8 +479,7 @@
 
     attn_grad = whole(attn_pieces)
     mlp_grad = whole(mlp_pieces)
-    summed = lax.psum(jnp.concatenate(gain_grads, axis=0), ("section", "dp", "tensor"))
-    shard = norm_gains.shape[1]
+    summed = butterfly(jnp.concatenate(gain_grads, axis=0), ("tensor", "section", "dp"))
     gain_grad = lax.dynamic_slice(
         summed, (2 * section, lax.axis_index("dp") * shard), (2, shard)
     ).T[None]

time: 500 us -> 531 us (1.062)
  blocking collectives: 38.9 us -> 0 us
  matrix products: 57 us -> 94.5 us
  starting transfers between devices: 61.8 us -> 79.6 us
  local copies, waits for them, and re-layouts: 36.2 us -> 47.4 us
  waiting for transfers between devices: 176 us -> 185 us
    psum x1 -> x0, blocking collectives: 38.9 us -> none  [local_program(): lax.psum(jnp.concatenate(gain_grads, axis=0), ('section', 'dp', 'tensor'))]
    dot_general x24 -> x72, matrix products: 57 us -> 94.5 us  [the longest x32 42.6 us: product_back(): lax.dot_general(block, weight, NT, preferred_element_type=F32)]
    ppermute x4 -> x21, waiting for transfers between devices: 0.27 us -> 35.8 us  [over(): return lax.ppermute(value, axis, [(i, i ^ by) for i in range(count)])]
    all_gather x1, waiting for transfers between devices: 33.2 us -> 0.01 us  [local_program(): second = lax.all_gather(second, ('section', 'dp'), axis=0, tiled=True)]
    ppermute x4 -> x21, starting transfers between devices: 0.43 us -> 19.9 us  [over(): return lax.ppermute(value, axis, [(i, i ^ by) for i in range(count)])]
    dynamic_update_slice x0 -> x5, local copies, waits for them, and re-layouts: none -> 10.6 us  [the longest x4 10.3 us: dp_gather(): full = lax.dynamic_update_slice_in_dim(full, block, (index ^ by) * rows, 0)]
    convert_element_type x2 -> x8, local copies, waits for them, and re-layouts: 2.02 us -> 9.66 us  [low(): return [block.astype(BF16) for block in blocks]]
    ppermute x48, waiting for transfers between devices: 142 us -> 149 us  [exchange(): return lax.ppermute(value, 'tensor', [(i, i ^ by) for i in range(count)])]
  transfers between devices with their start and end apart: 58 -> 74, of which waited for: 29 -> 36; matrix products, arithmetic and copies ran while one was open for 20% -> 31% of each run, Pallas kernels for 10% -> 10%
where the time goes in v2:
time: 531 us; the launch traced here: 525 us
  waiting for transfers between devices  185 us (35%)
  matrix products  94.5 us (18%)
  starting transfers between devices  79.6 us (15%)
  Pallas kernels  69.6 us (13%)
  local copies, waits for them, and re-layouts  47.4 us (9%)
  other arithmetic  33.3 us (6%)
  between operations  16.1 us (3%)
    ppermute x48, waiting for transfers between devices, exchange(): return lax.ppermute(value, 'tensor', [(i, i ^ by) for i in range(count)])  149 us
    ppermute x48, starting transfers between devices, exchange(): return lax.ppermute(value, 'tensor', [(i, i ^ by) for i in range(count)])  58.7 us
    dot_general x32, matrix products, product_back(): lax.dot_general(block, weight, NT, preferred_element_type=F32)  42.6 us
    dot_general x32, matrix products, product(): jnp.dot(block, weight, preferred_element_type=F32)  38 us
    pallas_call x2, Pallas kernels, attend_back(): pl.pallas_call(functools.partial(attend_back_kernel, local=local, own=own...  37.1 us
    ppermute x21, waiting for transfers between devices, over(): return lax.ppermute(value, axis, [(i, i ^ by) for i in range(count)])  35.8 us
    pallas_call x2, Pallas kernels, attend(): pl.pallas_call(functools.partial(attend_kernel, local=local, own=own, dev...  32.5 us
    unnamed x231, local copies, waits for them, and re-layouts  21.9 us
  transfers between devices with their start and end apart: 74, of which 36 were waited for; matrix products, arithmetic and copies ran while one was open for 31% of the time, Pallas kernels for 10%

profile of v2, /device:TPU:0, one launch (start us, length us, event | category | flops | bytes accessed | tf_op | source)
XLA Modules:
  0.0 525.5 jit_solution(2413447076926892780)
XLA Ops:
  14.5 5.0 collective-permute-start.6
  23.1 9.7 %collective-permute-done.4 = bf16[192,384]{0,1:T(8,128)(2,1)S(1)} collective-permute-done((bf16[192,384]{0,1:T(8,128)(2,1)S(1)}, bf16[192,384]{0,1:T(8,128)(2,1)S(1)}, u32[]{:S(2)}, u32[]{:S(2)}) %collective-permute-start.4) | collective-permute-done | bytes 147488 | tf_op jit(solution)/shard_map/ppermute | solution.py:50
  62.8 14.5 %collective-permute-done.8 = bf16[256,768]{1,0:T(8,128)(2,1)S(1)} collective-permute-done((bf16[256,768]{1,0:T(8,128)(2,1)S(1)}, bf16[256,768]{1,0:T(8,128)(2,1)S(1)}, u32[]{:S(2)}, u32[]{:S(2)}) %collective-permute-start.8) | collective-permute-done | bytes 393248 | tf_op jit(solution)/shard_map/ppermute | solution.py:33
  81.5 14.3 %attend.2 = (bf16[3,1024,64]{2,1,0:T(8,128)(2,1)}, bf16[3,1024,64]{2,1,0:T(8,128)(2,1)}, bf16[3,1024,64]{2,1,0:T(8,128)(2,1)}, bf16[1024,192]{1,0:T(8,128)(2,1)}, f32[3,8,1024]{2,1,0:T(8,128)}) custom-call(s32[2]{0:T(128)} %pad_add_fusion.scalars, f32[1024,64]{1,0:T(8,128)} %get-tuple-element.162.cosine, f32[1024,64]{1,0:T(8,128)} %get-tuple-element.163.sine, ...), custom_call_target="tpu_custom_call" | custom-call | tf_op jit(solution)/shard_map/attend/pallas_call | solution.py:196
  102.8 8.5 %collective-permute-done.11 = bf16[256,768]{1,0:T(8,128)(2,1)S(1)} collective-permute-done((bf16[256,768]{1,0:T(8,128)(2,1)S(1)}, bf16[256,768]{1,0:T(8,128)(2,1)S(1)}, u32[]{:S(2)}, u32[]{:S(2)}) %collective-permute-start.11) | collective-permute-done | bytes 393248 | tf_op jit(solution)/shard_map/ppermute | solution.py:33
  111.3 7.3 %collective-permute-done.12 = bf16[256,768]{1,0:T(8,128)(2,1)S(1)} collective-permute-done((bf16[256,768]{1,0:T(8,128)(2,1)S(1)}, bf16[256,768]{1,0:T(8,128)(2,1)S(1)}, u32[]{:S(2)}, u32[]{:S(2)}) %collective-permute-start.12) | collective-permute-done | bytes 393248 | tf_op jit(solution)/shard_map/ppermute | solution.py:33
  125.8 7.4 %collective-permute-done.14 = bf16[256,768]{1,0:T(8,128)(2,1)S(1)} collective-permute-done((bf16[256,768]{1,0:T(8,128)(2,1)S(1)}, bf16[256,768]{1,0:T(8,128)(2,1)S(1)}, u32[]{:S(2)}, u32[]{:S(2)}) %collective-permute-start.14) | collective-permute-done | bytes 393248 | tf_op jit(solution)/shard_map/ppermute | solution.py:33
  153.5 6.2 %collective-permute-done.17 = bf16[256,768]{1,0:T(8,128)(2,1)S(1)} collective-permute-done((bf16[256,768]{1,0:T(8,128)(2,1)S(1)}, bf16[256,768]{1,0:T(8,128)(2,1)S(1)}, u32[]{:S(2)}, u32[]{:S(2)}) %collective-permute-start.17) | collective-permute-done | bytes 393248 | tf_op jit(solution)/shard_map/ppermute | solution.py:33
  174.9 6.6 %collective-permute-done.21 = bf16[256,768]{1,0:T(8,128)(2,1)S(1)} collective-permute-done((bf16[256,768]{1,0:T(8,128)(2,1)S(1)}, bf16[256,768]{1,0:T(8,128)(2,1)S(1)}, u32[]{:S(2)}, u32[]{:S(2)}) %collective-permute-start.21) | collective-permute-done | bytes 393248 | tf_op jit(solution)/shard_map/ppermute | solution.py:33
  184.2 18.2 %attend.3 = (bf16[3,1024,64]{2,1,0:T(8,128)(2,1)}, bf16[3,1024,64]{2,1,0:T(8,128)(2,1)}, bf16[3,1024,64]{2,1,0:T(8,128)(2,1)}, bf16[1024,192]{1,0:T(8,128)(2,1)}, f32[3,8,1024]{2,1,0:T(8,128)}) custom-call(s32[2]{0:T(128)} %pad_add_fusion.scalars, f32[1024,64]{1,0:T(8,128)} %get-tuple-element.164.cosine, f32[1024,64]{1,0:T(8,128)} %get-tuple-element.165.sine, ...), custom_call_target="tpu_custom_call" | custom-call | tf_op jit(solution)/shard_map/attend/pallas_call | solution.py:196
  217.2 14.6 %collective-permute-done.24 = bf16[256,768]{1,0:T(8,128)(2,1)S(1)} collective-permute-done((bf16[256,768]{1,0:T(8,128)(2,1)S(1)}, bf16[256,768]{1,0:T(8,128)(2,1)S(1)}, u32[]{:S(2)}, u32[]{:S(2)}) %collective-permute-start.24) | collective-permute-done | bytes 393248 | tf_op jit(solution)/shard_map/ppermute | solution.py:33
  238.0 8.7 %collective-permute-done.30 = bf16[256,768]{1,0:T(8,128)(2,1)S(1)} collective-permute-done((bf16[256,768]{1,0:T(8,128)(2,1)S(1)}, bf16[256,768]{1,0:T(8,128)(2,1)S(1)}, u32[]{:S(2)}, u32[]{:S(2)}) %collective-permute-start.30) | collective-permute-done | bytes 393248 | tf_op jit(solution)/shard_map/ppermute | solution.py:33
  275.8 8.8 %collective-permute-done.36 = bf16[256,768]{1,0:T(8,128)(2,1)} collective-permute-done((bf16[256,768]{1,0:T(8,128)(2,1)}, bf16[256,768]{1,0:T(8,128)(2,1)}, u32[]{:S(2)}, u32[]{:S(2)}) %collective-permute-start.36) | collective-permute-done | bytes 393248 | tf_op jit(solution)/shard_map/ppermute | solution.py:33
  315.4 22.0 %attend_back.2 = bf16[1024,576]{1,0:T(8,128)(2,1)} custom-call(s32[2]{0:T(128)} %pad_add_fusion.scalars, bf16[3,1024,64]{2,1,0:T(8,128)(2,1)} %get-tuple-element.30.q3, bf16[3,1024,64]{2,1,0:T(8,128)(2,1)} %get-tuple-element.31.k3, bf16[3,1024,64]{2,1,0:T(8,128)(2,1)} %get-tuple-element.32.v3, f32[3,8,1024]{2,1,0:T(8,128)} %get-tuple-element.33.lse, ...), custom_call_target="tpu_custom_call" | custom-call | tf_op jit(solution)/shard_map/attend_back/pallas_call | solution.py:280
  354.2 7.7 %collective-permute-done.43 = bf16[256,768]{1,0:T(8,128)(2,1)} collective-permute-done((bf16[256,768]{1,0:T(8,128)(2,1)}, bf16[256,768]{1,0:T(8,128)(2,1)}, u32[]{:S(2)}, u32[]{:S(2)}) %collective-permute-start.43) | collective-permute-done | bytes 393248 | tf_op jit(solution)/shard_map/ppermute | solution.py:33
  371.5 6.7 %collective-permute-done.49 = bf16[256,768]{1,0:T(8,128)(2,1)S(1)} collective-permute-done((bf16[256,768]{1,0:T(8,128)(2,1)S(1)}, bf16[256,768]{1,0:T(8,128)(2,1)S(1)}, u32[]{:S(2)}, u32[]{:S(2)}) %collective-permute-start.49) | collective-permute-done | bytes 393248 | tf_op jit(solution)/shard_map/ppermute | solution.py:33
  380.8 5.7 %collective-permute-done.47 = bf16[256,768]{1,0:T(8,128)(2,1)S(1)} collective-permute-done((bf16[256,768]{1,0:T(8,128)(2,1)S(1)}, bf16[256,768]{1,0:T(8,128)(2,1)S(1)}, u32[]{:S(2)}, u32[]{:S(2)}) %collective-permute-start.47) | collective-permute-done | bytes 393248 | tf_op jit(solution)/shard_map/ppermute | solution.py:33
  393.6 7.8 %collective-permute-done.48 = bf16[256,768]{1,0:T(8,128)(2,1)S(1)} collective-permute-done((bf16[256,768]{1,0:T(8,128)(2,1)S(1)}, bf16[256,768]{1,0:T(8,128)(2,1)S(1)}, u32[]{:S(2)}, u32[]{:S(2)}) %collective-permute-start.48) | collective-permute-done | bytes 393248 | tf_op jit(solution)/shard_map/ppermute | solution.py:33
  409.2 7.0 %collective-permute-done.53 = bf16[256,768]{1,0:T(8,128)(2,1)S(1)} collective-permute-done((bf16[256,768]{1,0:T(8,128)(2,1)S(1)}, bf16[256,768]{1,0:T(8,128)(2,1)S(1)}, u32[]{:S(2)}, u32[]{:S(2)}) %collective-permute-start.53) | collective-permute-done | bytes 393248 | tf_op jit(solution)/shard_map/ppermute | solution.py:33
  417.2 6.1 %collective-permute-done.52 = bf16[256,768]{1,0:T(8,128)(2,1)S(1)} collective-permute-done((bf16[256,768]{1,0:T(8,128)(2,1)S(1)}, bf16[256,768]{1,0:T(8,128)(2,1)S(1)}, u32[]{:S(2)}, u32[]{:S(2)}) %collective-permute-start.52) | collective-permute-done | bytes 393248 | tf_op jit(solution)/shard_map/ppermute | solution.py:33
  426.4 15.1 %attend_back.3 = bf16[1024,576]{1,0:T(8,128)(2,1)} custom-call(s32[2]{0:T(128)} %pad_add_fusion.scalars, bf16[3,1024,64]{2,1,0:T(8,128)(2,1)} %get-tuple-element.26.q3, bf16[3,1024,64]{2,1,0:T(8,128)(2,1)} %get-tuple-element.27.k3, bf16[3,1024,64]{2,1,0:T(8,128)(2,1)} %get-tuple-element.28.v3, f32[3,8,1024]{2,1,0:T(8,128)} %get-tuple-element.29.lse, ...), custom_call_target="tpu_custom_call" | custom-call | tf_op jit(solution)/shard_map/attend_back/pallas_call | solution.py:280
  456.2 8.8 %collective-permute-done.55 = bf16[256,768]{1,0:T(8,128)(2,1)} collective-permute-done((bf16[256,768]{1,0:T(8,128)(2,1)}, bf16[256,768]{1,0:T(8,128)(2,1)}, u32[]{:S(2)}, u32[]{:S(2)}) %collective-permute-start.55) | collective-permute-done | bytes 393248 | tf_op jit(solution)/shard_map/ppermute | solution.py:33
  493.8 6.0 %collective-permute-done.61 = bf16[192,384]{0,1:T(8,128)(2,1)S(1)} collective-permute-done((bf16[192,384]{0,1:T(8,128)(2,1)S(1)}, bf16[192,384]{0,1:T(8,128)(2,1)S(1)}, u32[]{:S(2)}, u32[]{:S(2)}) %collective-permute-start.61) | collective-permute-done | bytes 147488 | tf_op jit(solution)/shard_map/ppermute | solution.py:50
  499.8 7.5 %collective-permute-done.60 = bf16[192,384]{0,1:T(8,128)(2,1)} collective-permute-done((bf16[192,384]{0,1:T(8,128)(2,1)S(1)}, bf16[192,384]{0,1:T(8,128)(2,1)}, u32[]{:S(2)}, u32[]{:S(2)}) %collective-permute-start.60) | collective-permute-done | bytes 147488 | tf_op jit(solution)/shard_map/ppermute | solution.py:50
  (551 shorter events, 279.1 us)
Async XLA Ops:
  7.2 126.0 %all-gather.3.cloned.1.call-start = ((), (), s32[]{:S(2)}) async-start(), calls=%async_computation.3 | async-start | bytes 3096576 | tf_op jit(solution)/shard_map/all_gather | solution.py:412
  8.3 40.3 %collective-permute-start = (f32[4,768]{1,0:T(4,128)S(1)}, f32[4,768]{1,0:T(4,128)S(1)}, u32[]{:S(2)}, u32[]{:S(2)}) collective-permute-start(f32[4,768]{1,0:T(4,128)S(1)} %dynamic_update_slice.17), channel_id=1, source_target_pairs={{0,16},{16,0},{1,17},{17,1},{2,18},{18,2},{3,19},{19,3},{4,20},{20... | collective-permute-start | bytes 36872 | tf_op jit(solution)/shard_map/ppermute | solution.py:50
  14.5 24.3 %collective-permute-start.6 = (bf16[192,384]{0,1:T(8,128)(2,1)S(1)}, bf16[192,384]{0,1:T(8,128)(2,1)S(1)}, u32[]{:S(2)}, u32[]{:S(2)}) collective-permute-start(bf16[192,384]{0,1:T(8,128)(2,1)S(1)} %get-tuple-element.137), channel_id=1, source_target_pairs={{0,12},{4,8},{8,4},{12,0},{1,13},{5,9},{9,5},{13,1},{2,14},{6,10},... | collective-permute-start | bytes 442376 | tf_op jit(solution)/shard_map/ppermute | solution.py:50
  48.1 119.0 %all-gather.5.cloned.1.call-start = ((), (), s32[]{:S(2)}) async-start(), calls=%async_computation.4 | async-start | bytes 1327104 | tf_op jit(solution)/shard_map/all_gather | solution.py:413
  57.7 22.4 %collective-permute-start.10 = (bf16[256,768]{1,0:T(8,128)(2,1)S(1)}, bf16[256,768]{1,0:T(8,128)(2,1)S(1)}, u32[]{:S(2)}, u32[]{:S(2)}) collective-permute-start(bf16[256,768]{1,0:T(8,128)(2,1)S(1)} %fusion.151), channel_id=1, source_target_pairs={{0,3},{1,2},{2,1},{3,0},{4,7},{5,6},{6,5},{7,4},{8,11},{9,10},{10,... | collective-permute-start | bytes 1179656 | tf_op jit(solution)/shard_map/ppermute | solution.py:33
  122.5 365.6 %reduce-scatter.14.cloned.1.call-start = ((), (), s32[]{:S(2)}) async-start(), calls=%async_computation.7 | async-start | bytes 1769472
  122.8 24.2 %collective-permute-start.18 = (bf16[256,768]{1,0:T(8,128)(2,1)S(1)}, bf16[256,768]{1,0:T(8,128)(2,1)}, u32[]{:S(2)}, u32[]{:S(2)}) collective-permute-start(bf16[256,768]{1,0:T(8,128)(2,1)S(1)} %multiply_convert_fusion.1), channel_id=1, source_target_pairs={{0,3},{1,2},{2,1},{3,0},{4,7},{5,6},{6,5},{7,4},{8,11},{9,10},{10,... | collective-permute-start | bytes 1179656 | tf_op jit(solution)/shard_map/ppermute | solution.py:33
  206.6 25.1 %collective-permute-start.24 = (bf16[256,768]{1,0:T(8,128)(2,1)S(1)}, bf16[256,768]{1,0:T(8,128)(2,1)S(1)}, u32[]{:S(2)}, u32[]{:S(2)}) collective-permute-start(bf16[256,768]{1,0:T(8,128)(2,1)S(1)} %convolution_convert_fusion.17), channel_id=1, source_target_pairs={{0,2},{1,3},{2,0},{3,1},{4,6},{5,7},{6,4},{7,5},{8,10},{9,11},{10,... | collective-permute-start | bytes 1179656 | tf_op jit(solution)/shard_map/ppermute | solution.py:33
  208.8 23.0 %collective-permute-start.25 = (bf16[256,768]{1,0:T(8,128)(2,1)S(1)}, bf16[256,768]{1,0:T(8,128)(2,1)S(1)}, u32[]{:S(2)}, u32[]{:S(2)}) collective-permute-start(bf16[256,768]{1,0:T(8,128)(2,1)S(1)} %convolution_convert_fusion.16), channel_id=1, source_target_pairs={{0,3},{1,2},{2,1},{3,0},{4,7},{5,6},{6,5},{7,4},{8,11},{9,10},{10,... | collective-permute-start | bytes 1179656 | tf_op jit(solution)/shard_map/ppermute | solution.py:33
  210.5 37.7 %collective-permute-start.37 = (bf16[256,768]{1,0:T(8,128)(2,1)S(1)}, bf16[256,768]{1,0:T(8,128)(2,1)S(1)}, u32[]{:S(2)}, u32[]{:S(2)}) collective-permute-start(bf16[256,768]{1,0:T(8,128)(2,1)S(1)} %dynamic-slice_bitcast_fusion), channel_id=1, source_target_pairs={{0,3},{1,2},{2,1},{3,0},{4,7},{5,6},{6,5},{7,4},{8,11},{9,10},{10,... | collective-permute-start | bytes 1179656 | tf_op jit(solution)/shard_map/ppermute | solution.py:33
  211.9 43.7 %collective-permute-start.35 = (bf16[256,768]{1,0:T(8,128)(2,1)S(1)}, bf16[256,768]{1,0:T(8,128)(2,1)S(1)}, u32[]{:S(2)}, u32[]{:S(2)}) collective-permute-start(bf16[256,768]{1,0:T(8,128)(2,1)S(1)} %dynamic-slice_bitcast_fusion), channel_id=1, source_target_pairs={{0,2},{1,3},{2,0},{3,1},{4,6},{5,7},{6,4},{7,5},{8,10},{9,11},{10,... | collective-permute-start | bytes 1179656 | tf_op jit(solution)/shard_map/ppermute | solution.py:33
  216.1 46.6 %collective-permute-start.33 = (bf16[256,768]{1,0:T(8,128)(2,1)S(1)}, bf16[256,768]{1,0:T(8,128)(2,1)S(1)}, u32[]{:S(2)}, u32[]{:S(2)}) collective-permute-start(bf16[256,768]{1,0:T(8,128)(2,1)S(1)} %dynamic-slice_bitcast_fusion), channel_id=1, source_target_pairs={{0,1},{1,0},{2,3},{3,2},{4,5},{5,4},{6,7},{7,6},{8,9},{9,8},{10,11... | collective-permute-start | bytes 1179656 | tf_op jit(solution)/shard_map/ppermute | solution.py:33
  235.4 19.6 %collective-permute-start.28 = (bf16[256,768]{1,0:T(8,128)(2,1)S(1)}, bf16[256,768]{1,0:T(8,128)(2,1)S(1)}, u32[]{:S(2)}, u32[]{:S(2)}) collective-permute-start(bf16[256,768]{1,0:T(8,128)(2,1)S(1)} %multiply_convert_fusion), channel_id=1, source_target_pairs={{0,2},{1,3},{2,0},{3,1},{4,6},{5,7},{6,4},{7,5},{8,10},{9,11},{10,... | collective-permute-start | bytes 1179656 | tf_op jit(solution)/shard_map/ppermute | solution.py:33
  250.9 39.9 %collective-permute-start.31 = (bf16[256,768]{1,0:T(8,128)(2,1)}, bf16[256,768]{1,0:T(8,128)(2,1)}, u32[]{:S(2)}, u32[]{:S(2)}) collective-permute-start(bf16[256,768]{1,0:T(8,128)(2,1)} %convolution_convert_fusion.24), channel_id=1, source_target_pairs={{0,3},{1,2},{2,1},{3,0},{4,7},{5,6},{6,5},{7,4},{8,11},{9,10},{10,... | collective-permute-start | bytes 1179656 | tf_op jit(solution)/shard_map/ppermute | solution.py:33
  258.3 33.5 %collective-permute-start.29 = (bf16[256,768]{1,0:T(8,128)(2,1)}, bf16[256,768]{1,0:T(8,128)(2,1)}, u32[]{:S(2)}, u32[]{:S(2)}) collective-permute-start(bf16[256,768]{1,0:T(8,128)(2,1)} %convolution_convert_fusion.25), channel_id=1, source_target_pairs={{0,2},{1,3},{2,0},{3,1},{4,6},{5,7},{6,4},{7,5},{8,10},{9,11},{10,... | collective-permute-start | bytes 1179656 | tf_op jit(solution)/shard_map/ppermute | solution.py:33
  262.1 22.4 %collective-permute-start.36 = (bf16[256,768]{1,0:T(8,128)(2,1)}, bf16[256,768]{1,0:T(8,128)(2,1)}, u32[]{:S(2)}, u32[]{:S(2)}) collective-permute-start(bf16[256,768]{1,0:T(8,128)(2,1)} %convolution_convert_fusion.13), channel_id=1, source_target_pairs={{0,2},{1,3},{2,0},{3,1},{4,6},{5,7},{6,4},{7,5},{8,10},{9,11},{10,... | collective-permute-start | bytes 1179656 | tf_op jit(solution)/shard_map/ppermute | solution.py:33
  272.0 217.9 %reduce-scatter.10.cloned.1.call-start = ((), (), s32[]{:S(2)}) async-start(), calls=%async_computation.5 | async-start | bytes 1327104
  290.8 20.6 %collective-permute-start.39 = (bf16[256,768]{1,0:T(8,128)(2,1)S(1)}, bf16[256,768]{1,0:T(8,128)(2,1)}, u32[]{:S(2)}, u32[]{:S(2)}) collective-permute-start(bf16[256,768]{1,0:T(8,128)(2,1)S(1)} %fusion.171), channel_id=1, source_target_pairs={{0,1},{1,0},{2,3},{3,2},{4,5},{5,4},{6,7},{7,6},{8,9},{9,8},{10,11... | collective-permute-start | bytes 1179656 | tf_op jit(solution)/shard_map/ppermute | solution.py:33
  294.5 71.9 %collective-permute-start.32 = (bf16[256,768]{1,0:T(8,128)(2,1)}, bf16[256,768]{1,0:T(8,128)(2,1)}, u32[]{:S(2)}, u32[]{:S(2)}) collective-permute-start(bf16[256,768]{1,0:T(8,128)(2,1)} %get-tuple-element.154), channel_id=1, source_target_pairs={{0,16},{16,0},{1,17},{17,1},{2,18},{18,2},{3,19},{19,3},{4,20},{20... | collective-permute-start | bytes 1179656 | tf_op jit(solution)/shard_map/ppermute | solution.py:50
  353.8 157.0 %reduce-scatter.12.cloned.1.call-start = ((), (), s32[]{:S(2)}) async-start(), calls=%async_computation.6 | async-start | bytes 1769472
  369.7 19.7 %collective-permute-start.45 = (bf16[256,768]{1,0:T(8,128)(2,1)S(1)}, bf16[256,768]{1,0:T(8,128)(2,1)S(1)}, u32[]{:S(2)}, u32[]{:S(2)}) collective-permute-start(bf16[256,768]{1,0:T(8,128)(2,1)S(1)} %add_convert_fusion.2), channel_id=1, source_target_pairs={{0,1},{1,0},{2,3},{3,2},{4,5},{5,4},{6,7},{7,6},{8,9},{9,8},{10,11... | collective-permute-start | bytes 1179656 | tf_op jit(solution)/shard_map/ppermute | solution.py:33
  445.4 19.7 %collective-permute-start.55 = (bf16[256,768]{1,0:T(8,128)(2,1)}, bf16[256,768]{1,0:T(8,128)(2,1)}, u32[]{:S(2)}, u32[]{:S(2)}) collective-permute-start(bf16[256,768]{1,0:T(8,128)(2,1)} %convolution_convert_fusion.1), channel_id=1, source_target_pairs={{0,2},{1,3},{2,0},{3,1},{4,6},{5,7},{6,4},{7,5},{8,10},{9,11},{10,... | collective-permute-start | bytes 1179656 | tf_op jit(solution)/shard_map/ppermute | solution.py:33
  478.1 30.5 %collective-permute-start.57 = (bf16[256,768]{1,0:T(8,128)(2,1)}, bf16[256,768]{1,0:T(8,128)(2,1)}, u32[]{:S(2)}, u32[]{:S(2)}) collective-permute-start(bf16[256,768]{1,0:T(8,128)(2,1)} %get-tuple-element.78), channel_id=1, source_target_pairs={{0,16},{16,0},{1,17},{17,1},{2,18},{18,2},{3,19},{19,3},{4,20},{20... | collective-permute-start | bytes 1179656 | tf_op jit(solution)/shard_map/ppermute | solution.py:50
  486.4 20.9 %collective-permute-start.60 = (bf16[192,384]{0,1:T(8,128)(2,1)S(1)}, bf16[192,384]{0,1:T(8,128)(2,1)}, u32[]{:S(2)}, u32[]{:S(2)}) collective-permute-start(bf16[192,384]{0,1:T(8,128)(2,1)S(1)} %get-tuple-element.135), channel_id=1, source_target_pairs={{0,8},{4,12},{8,0},{12,4},{1,9},{5,13},{9,1},{13,5},{2,10},{6,14},... | collective-permute-start | bytes 442376 | tf_op jit(solution)/shard_map/ppermute | solution.py:50
  (158 other events, 1648.2 us)
Sparse Core Ops, SparseCore 0:
  48.2 36.0 all-gather.2
  122.7 22.3 all-gather.4
  272.1 40.0 reduce-scatter.13
  354.0 36.4 reduce-scatter.9
  451.7 42.1 reduce-scatter.11

commit v3 on v1

--- a/solution.py
+++ b/solution.py
@@ -47,6 +47,16 @@
     return total
 
 
+def butterfly(value, axes):
+    for axis in axes:
+        count = lax.axis_size(axis)
+        by = 1
+        while by < count:
+            value = value + lax.ppermute(value, axis, [(i, i ^ by) for i in range(count)])
+            by *= 2
+    return value
+
+
 def positions(own, devices):
     index = lax.axis_index("tensor")
     row = jnp.arange(own * devices, dtype=jnp.int32)
@@ -78,7 +88,7 @@
     return place, pl.multiple_of(before, HALF_WINDOW), pl.multiple_of(after, HALF_WINDOW)
 
 
-def attend_kernel(scalars, qkv, cosine, sine, q3, k3, v3, out, lse, *, local, own, devices, heads):
+def attend_kernel(scalars, qkv, cosine, sine, q3, k3, v3, out, lse, o3, *, local, own, devices, heads):
     count = own * devices
     width = heads * HEAD
     length = scalars[1]
@@ -88,57 +98,59 @@
             rows = qkv[:, part * width + at : part * width + at + HEAD]
             store[head] = (rows * cosine[...] + turn(rows) * sine[...]).astype(BF16)
         v3[head] = qkv[:, 2 * width + at : 2 * width + at + HEAD].astype(BF16)
+    def step(at, carry):
+        head = at // devices
+        block = at % devices
+        start = pl.multiple_of(block * own, own)
+        query = q3[head, pl.ds(start, own), :]
+        if local:
+            place, before, after = neighbours(scalars, block, own, devices)
+            key = jnp.concatenate(
+                [
+                    k3[head, pl.ds(before, HALF_WINDOW), :],
+                    k3[head, pl.ds(start, own), :],
+                    k3[head, pl.ds(after, HALF_WINDOW), :],
+                ],
+                axis=0,
+            )
+            value = jnp.concatenate(
+                [
+                    v3[head, pl.ds(before, HALF_WINDOW), :],
+                    v3[head, pl.ds(start, own), :],
+                    v3[head, pl.ds(after, HALF_WINDOW), :],
+                ],
+                axis=0,
+            )
+            span = own + 2 * HALF_WINDOW
+            shape = (own, span)
+            row = lax.broadcasted_iota(jnp.int32, shape, 0)
+            column = lax.broadcasted_iota(jnp.int32, shape, 1) - HALF_WINDOW
+            spot = column + place * own
+            near = jnp.abs(row - column) <= HALF_WINDOW
+            allowed = (near & (spot >= 0) & (spot < length)) | (row == column)
+        else:
+            key = k3[head]
+            value = v3[head]
+            shape = (own, count)
+            row = lax.broadcasted_iota(jnp.int32, shape, 0) + start
+            column = lax.broadcasted_iota(jnp.int32, shape, 1)
+            spot = ((column // own) ^ scalars[0]) * own + column % own
+            allowed = (spot < length) | (row == column)
+        raw = lax.dot_general(query, key, NT, preferred_element_type=F32) * SCALE
+        scores = jnp.where(allowed, raw, MASKED)
+        highest = jnp.max(scores, axis=1, keepdims=True)
+        lifted = jnp.exp(scores - highest)
+        summed = jnp.sum(lifted, axis=1, keepdims=True)
+        probs = (lifted / summed).astype(BF16)
+        got = jnp.dot(probs, value, preferred_element_type=F32)
+        o3[head, pl.ds(start, own), :] = got.astype(BF16)
+        total = jnp.broadcast_to(highest + jnp.log(summed), (own, 128))
+        lse[head, :, pl.ds(start, own)] = total.T[:8]
+        return carry
+
+    lax.fori_loop(0, heads * devices, step, 0)
     for head in range(heads):
-
-        def step(block, carry):
-            start = pl.multiple_of(block * own, own)
-            query = q3[head, pl.ds(start, own), :]
-            if local:
-                place, before, after = neighbours(scalars, block, own, devices)
-                key = jnp.concatenate(
-                    [
-                        k3[head, pl.ds(before, HALF_WINDOW), :],
-                        k3[head, pl.ds(start, own), :],
-                        k3[head, pl.ds(after, HALF_WINDOW), :],
-                    ],
-                    axis=0,
-                )
-                value = jnp.concatenate(
-                    [
-                        v3[head, pl.ds(before, HALF_WINDOW), :],
-                        v3[head, pl.ds(start, own), :],
-                        v3[head, pl.ds(after, HALF_WINDOW), :],
-                    ],
-                    axis=0,
-                )
-                span = own + 2 * HALF_WINDOW
-                shape = (own, span)
-                row = lax.broadcasted_iota(jnp.int32, shape, 0)
-                column = lax.broadcasted_iota(jnp.int32, shape, 1) - HALF_WINDOW
-                spot = column + place * own
-                near = jnp.abs(row - column) <= HALF_WINDOW
-                allowed = (near & (spot >= 0) & (spot < length)) | (row == column)
-            else:
-                key = k3[head]
-                value = v3[head]
-                shape = (own, count)
-                row = lax.broadcasted_iota(jnp.int32, shape, 0) + start
-                column = lax.broadcasted_iota(jnp.int32, shape, 1)
-                spot = ((column // own) ^ scalars[0]) * own + column % own
-                allowed = (spot < length) | (row == column)
-            raw = lax.dot_general(query, key, NT, preferred_element_type=F32) * SCALE
-            scores = jnp.where(allowed, raw, MASKED)
-            highest = jnp.max(scores, axis=1, keepdims=True)
-            lifted = jnp.exp(scores - highest)
-            summed = jnp.sum(lifted, axis=1, keepdims=True)
-            probs = (lifted / summed).astype(BF16)
-            got = jnp.dot(probs, value, preferred_element_type=F32)
-            out[pl.ds(start, own), head * HEAD : (head + 1) * HEAD] = got.astype(BF16)
-            total = jnp.broadcast_to(highest + jnp.log(summed), (own, 128))
-            lse[head, :, pl.ds(start, own)] = total.T[:8]
-            return carry
-
-        lax.fori_loop(0, devices, step, 0)
+        out[:, head * HEAD : (head + 1) * HEAD] = o3[head]
 
 
 def attend(qkv, cosine, sine, scalars, local, own, devices, heads):
@@ -156,70 +168,76 @@
         ),
         in_specs=[pl.BlockSpec(memory_space=pltpu.SMEM), vmem, vmem, vmem],
         out_specs=(vmem, vmem, vmem, vmem, vmem),
+        scratch_shapes=[pltpu.VMEM((heads, count, HEAD), BF16)],
         name="attend",
     )(scalars, qkv, cosine, sine)
 
 
 def attend_back_kernel(
-    scalars, q3, k3, v3, grad, lse, cosine, sine, out, dk, dv, *, local, own, devices, heads
+    scalars, q3, k3, v3, grad, lse, cosine, sine, out, dq, dk, dv, grad3, *, local, own, devices, heads
 ):
     count = own * devices
     width = heads * HEAD
     length = scalars[1]
+    dk[...] = jnp.zeros_like(dk)
+    dv[...] = jnp.zeros_like(dv)
     for head in range(heads):
-        dk[...] = jnp.zeros_like(dk)
-        dv[...] = jnp.zeros_like(dv)
-
-        def step(block, carry):
-            start = pl.multiple_of(block * own, own)
-            here = pl.ds(start, own)
-            query = q3[head, here, :]
-            upstream = grad[here, head * HEAD : (head + 1) * HEAD]
-            if local:
-                place, before, after = neighbours(scalars, block, own, devices)
-                pieces = (
-                    (pl.ds(before, HALF_WINDOW), 0, HALF_WINDOW),
-                    (here, HALF_WINDOW, HALF_WINDOW + own),
-                    (pl.ds(after, HALF_WINDOW), HALF_WINDOW + own, 2 * HALF_WINDOW + own),
-                )
-                key = jnp.concatenate([k3[head, piece, :] for piece, _, _ in pieces], axis=0)
-                value = jnp.concatenate([v3[head, piece, :] for piece, _, _ in pieces], axis=0)
-                shape = (own + 2 * HALF_WINDOW, own)
-                row = lax.broadcasted_iota(jnp.int32, shape, 1)
-                column = lax.broadcasted_iota(jnp.int32, shape, 0) - HALF_WINDOW
-                spot = column + place * own
-                near = jnp.abs(row - column) <= HALF_WINDOW
-                allowed = (near & (spot >= 0) & (spot < length)) | (row == column)
-            else:
-                pieces = ((slice(None), 0, count),)
-                key = k3[head]
-                value = v3[head]
-                shape = (count, own)
-                row = lax.broadcasted_iota(jnp.int32, shape, 1) + start
-                column = lax.broadcasted_iota(jnp.int32, shape, 0)
-                spot = ((column // own) ^ scalars[0]) * own + column % own
-                allowed = (spot < length) | (row == column)
-            raw = lax.dot_general(key, query, NT, preferred_element_type=F32) * SCALE
-            scores = jnp.where(allowed, raw, MASKED)
-            probs = jnp.exp(scores - lse[head, 0:1, here])
-            d_probs = lax.dot_general(value, upstream, NT, preferred_element_type=F32)
-            weighted = jnp.sum(probs * d_probs, axis=0, keepdims=True)
-            d_scores = (probs * (d_probs - weighted)).astype(BF16)
-            d_key = jnp.dot(d_scores, query, preferred_element_type=F32) * SCALE
-            d_value = jnp.dot(probs.astype(BF16), upstream, preferred_element_type=F32)
-            for piece, low, high in pieces:
-                dk[piece, :] += d_key[low:high]
-                dv[piece, :] += d_value[low:high]
-            d_query = jnp.dot(key.T, d_scores, preferred_element_type=F32).T * SCALE
-            d_query = d_query * cosine[here, :] - turn(d_query) * sine[here, :]
-            out[here, head * HEAD : (head + 1) * HEAD] = d_query.astype(BF16)
-            return carry
-
-        lax.fori_loop(0, devices, step, 0)
+        grad3[head] = grad[:, head * HEAD : (head + 1) * HEAD]
+
+    def step(at, carry):
+        head = at // devices
+        block = at % devices
+        start = pl.multiple_of(block * own, own)
+        here = pl.ds(start, own)
+        query = q3[head, here, :]
+        upstream = grad3[head, here, :]
+        if local:
+            place, before, after = neighbours(scalars, block, own, devices)
+            pieces = (
+                (pl.ds(before, HALF_WINDOW), 0, HALF_WINDOW),
+                (here, HALF_WINDOW, HALF_WINDOW + own),
+                (pl.ds(after, HALF_WINDOW), HALF_WINDOW + own, 2 * HALF_WINDOW + own),
+            )
+            key = jnp.concatenate([k3[head, piece, :] for piece, _, _ in pieces], axis=0)
+            value = jnp.concatenate([v3[head, piece, :] for piece, _, _ in pieces], axis=0)
+            shape = (own + 2 * HALF_WINDOW, own)
+            row = lax.broadcasted_iota(jnp.int32, shape, 1)
+            column = lax.broadcasted_iota(jnp.int32, shape, 0) - HALF_WINDOW
+            spot = column + place * own
+            near = jnp.abs(row - column) <= HALF_WINDOW
+            allowed = (near & (spot >= 0) & (spot < length)) | (row == column)
+        else:
+            pieces = ((slice(None), 0, count),)
+            key = k3[head]
+            value = v3[head]
+            shape = (count, own)
+            row = lax.broadcasted_iota(jnp.int32, shape, 1) + start
+            column = lax.broadcasted_iota(jnp.int32, shape, 0)
+            spot = ((column // own) ^ scalars[0]) * own + column % own
+            allowed = (spot < length) | (row == column)
+        raw = lax.dot_general(key, query, NT, preferred_element_type=F32) * SCALE
+        scores = jnp.where(allowed, raw, MASKED)
+        probs = jnp.exp(scores - lse[head, 0:1, here])
+        d_probs = lax.dot_general(value, upstream, NT, preferred_element_type=F32)
+        weighted = jnp.sum(probs * d_probs, axis=0, keepdims=True)
+        d_scores = (probs * (d_probs - weighted)).astype(BF16)
+        d_key = jnp.dot(d_scores, query, preferred_element_type=F32) * SCALE
+        d_value = jnp.dot(probs.astype(BF16), upstream, preferred_element_type=F32)
+        for piece, low, high in pieces:
+            dk[head, piece, :] += d_key[low:high]
+            dv[head, piece, :] += d_value[low:high]
+        d_query = jnp.dot(key.T, d_scores, preferred_element_type=F32).T * SCALE
+        d_query = d_query * cosine[here, :] - turn(d_query) * sine[here, :]
+        dq[head, here, :] = d_query.astype(BF16)
+        return carry
+
+    lax.fori_loop(0, heads * devices, step, 0)
+    for head in range(heads):
         at = head * HEAD
-        d_key = dk[...] * cosine[...] - turn(dk[...]) * sine[...]
+        d_key = dk[head] * cosine[...] - turn(dk[head]) * sine[...]
+        out[:, at : at + HEAD] = dq[head]
         out[:, width + at : width + at + HEAD] = d_key.astype(BF16)
-        out[:, 2 * width + at : 2 * width + at + HEAD] = dv[...].astype(BF16)
+        out[:, 2 * width + at : 2 * width + at + HEAD] = dv[head].astype(BF16)
 
 
 def attend_back(q3, k3, v3, grad, lse, cosine, sine, scalars, local, own, devices, heads):
@@ -230,7 +248,12 @@
         out_shape=jax.ShapeDtypeStruct((count, 3 * heads * HEAD), BF16),
         in_specs=[pl.BlockSpec(memory_space=pltpu.SMEM)] + [vmem] * 7,
         out_specs=vmem,
-        scratch_shapes=[pltpu.VMEM((count, HEAD), F32), pltpu.VMEM((count, HEAD), F32)],
+        scratch_shapes=[
+            pltpu.VMEM((heads, count, HEAD), BF16),
+            pltpu.VMEM((heads, count, HEAD), F32),
+            pltpu.VMEM((heads, count, HEAD), F32),
+            pltpu.VMEM((heads, count, HEAD), BF16),
+        ],
         name="attend_back",
     )(scalars, q3, k3, v3, grad, lse, cosine, sine)
 
@@ -279,11 +302,13 @@
     d_qkv = attend_back(
         q3, k3, v3, d_attended, lse, *tables, scalars, local, own, devices, heads
     )
+    grad_attn = jnp.concatenate(
+        [outer(rows_one, d_qkv).astype(BF16), outer(mixed_rows, attended).astype(BF16)], axis=1
+    )
+    if local:
+        grad_attn, d_qkv = lax.optimization_barrier((grad_attn, d_qkv))
     d_one = lax.dot_general(d_qkv, w_qkv, NT, preferred_element_type=F32)
     d_one = scatter_rows(d_one.astype(BF16))
-    grad_attn = jnp.concatenate(
-        [outer(rows_one, d_qkv).astype(BF16), outer(mixed_rows, attended).astype(BF16)], axis=1
-    )
     _, pull_first = jax.vjp(layer_norm, resid, gains[0])
     d_resid, gain_one = pull_first(d_one)
     return d_resid + d_mixed, grad_attn, grad_mlp, jnp.stack([gain_one, gain_two])
@@ -307,24 +332,30 @@
     units = w_gate.shape[2]
     swap = functools.partial(lax.ppermute, axis_name="section", perm=[(0, 1), (1, 0)])
 
-    attn_pack = jnp.concatenate([w_query, w_key, w_value, w_out, norm_gains], axis=2)[0]
+    attn_pack = jnp.concatenate([w_query, w_key, w_value, w_out], axis=2)[0]
     mlp_pack = jnp.concatenate([w_gate, w_up, w_down], axis=2)[0]
     attn_all = lax.all_gather(attn_pack, ("section", "dp"), axis=0, tiled=True)
     mlp_all = lax.all_gather(mlp_pack, ("section", "dp"), axis=0, tiled=True)
+    shard = norm_gains.shape[1]
+    spread = lax.dynamic_update_slice(
+        jnp.zeros((4, features), F32),
+        norm_gains[0].astype(F32).T,
+        (2 * section, lax.axis_index("dp") * shard),
+    )
+    all_gains = butterfly(spread, ("section", "dp"))
     weights = []
-    gains = []
+    gains = [all_gains[:2], all_gains[2:]]
     for layer in range(2):
         attn = attn_all[layer * features : (layer + 1) * features]
         mlp = mlp_all[layer * features : (layer + 1) * features]
         weights.append(
             (
                 attn[:, : 3 * head_width],
-                attn[:, 3 * head_width : 4 * head_width],
+                attn[:, 3 * head_width :],
                 mlp[:, : 2 * units],
                 mlp[:, 2 * units :],
             )
         )
-        gains.append(attn[:, 4 * head_width :].astype(F32).T)
 
     position = positions(own, devices)
     tables = [rotary_tables(position, theta) for theta in THETAS]
@@ -379,8 +410,7 @@
 
     attn_grad = whole(attn_pieces)
     mlp_grad = whole(mlp_pieces)
-    summed = lax.psum(jnp.concatenate(gain_grads, axis=0), ("section", "dp", "tensor"))
-    shard = norm_gains.shape[1]
+    summed = butterfly(jnp.concatenate(gain_grads, axis=0), ("tensor", "section", "dp"))
     gain_grad = lax.dynamic_slice(
         summed, (2 * section, lax.axis_index("dp") * shard), (2, shard)
     ).T[None]

time: 500 us -> 531 us (1.062)
  waiting for transfers between devices: 176 us -> 239 us
  blocking collectives: 38.9 us -> 0 us
  starting transfers between devices: 61.8 us -> 67.8 us
    ppermute x48, waiting for transfers between devices: 142 us -> 213 us  [exchange(): return lax.ppermute(value, 'tensor', [(i, i ^ by) for i in range(count)])]
    psum x1 -> x0, blocking collectives: 38.9 us -> none  [local_program(): lax.psum(jnp.concatenate(gain_grads, axis=0), ('section', 'dp', 'tensor'))]
    all_gather x1, waiting for transfers between devices: 33.2 us -> 2.02 us  [local_program(): attn_all = lax.all_gather(attn_pack, ('section', 'dp'), axis=0, tiled=True)]
    unnamed x10, waiting for transfers between devices: 0.16 us -> 16.3 us
    ppermute x0 -> x8, starting transfers between devices: none -> 10.9 us  [butterfly(): lax.ppermute(value, axis, [(i, i ^ by) for i in range(count)])]
    ppermute x0 -> x8, waiting for transfers between devices: none -> 8.08 us  [butterfly(): lax.ppermute(value, axis, [(i, i ^ by) for i in range(count)])]
    unnamed x179 -> x190, local copies, waits for them, and re-layouts: 24.3 us -> 26.8 us
  transfers between devices with their start and end apart: 58 -> 66, of which waited for: 29 -> 48; matrix products, arithmetic and copies ran while one was open for 20% -> 18% of each run, Pallas kernels for 10% -> 10%
where the time goes in v3:
time: 531 us; the launch traced here: 522 us
  waiting for transfers between devices  239 us (45%)
  starting transfers between devices  67.8 us (13%)
  Pallas kernels  67.3 us (13%)
  matrix products  57.8 us (11%)
  other arithmetic  39.9 us (8%)
  local copies, waits for them, and re-layouts  33.4 us (6%)
  between operations  15.9 us (3%)
    ppermute x48, waiting for transfers between devices, exchange(): return lax.ppermute(value, 'tensor', [(i, i ^ by) for i in range(count)])  213 us
    ppermute x48, starting transfers between devices, exchange(): return lax.ppermute(value, 'tensor', [(i, i ^ by) for i in range(count)])  55.6 us
    pallas_call x2, Pallas kernels, attend_back(): pl.pallas_call(functools.partial(attend_back_kernel, local=local, own=own...  36.7 us
    pallas_call x2, Pallas kernels, attend(): pl.pallas_call(functools.partial(attend_kernel, local=local, own=own, dev...  30.6 us
    unnamed x190, local copies, waits for them, and re-layouts  26.8 us
    unnamed x10, waiting for transfers between devices  16.3 us
    ppermute x8, starting transfers between devices, butterfly(): lax.ppermute(value, axis, [(i, i ^ by) for i in range(count)])  10.9 us
  transfers between devices with their start and end apart: 66, of which 48 were waited for; matrix products, arithmetic and copies ran while one was open for 18% of the time, Pallas kernels for 10%

profile of v3, /device:TPU:0, one launch (start us, length us, event | category | flops | bytes accessed | tf_op | source)
XLA Modules:
  0.0 521.5 jit_solution(3234939801727054965)
XLA Ops:
  36.7 5.9 %collective-permute-done.4 = bf16[256,768]{0,1:T(8,128)(2,1)S(1)} collective-permute-done((bf16[256,768]{0,1:T(8,128)(2,1)S(1)}, bf16[256,768]{0,1:T(8,128)(2,1)S(1)}, u32[]{:S(2)}, u32[]{:S(2)}) %collective-permute-start.4) | collective-permute-done | bytes 393248 | tf_op jit(solution)/shard_map/ppermute | solution.py:33
  48.8 13.2 %attend.2 = (bf16[3,1024,64]{2,1,0:T(8,128)(2,1)}, bf16[3,1024,64]{2,1,0:T(8,128)(2,1)}, bf16[3,1024,64]{2,1,0:T(8,128)(2,1)}, bf16[1024,192]{1,0:T(8,128)(2,1)}, f32[3,8,1024]{2,1,0:T(8,128)}) custom-call(s32[2]{0:T(128)} %pad_add_fusion.scalars, f32[1024,576]{1,0:T(8,128)} %fusion.41.qkv, f32[1024,64]{1,0:T(8,128)} %get-tuple-element.150.cosine, ...), custom_call_target="tpu_custom_call" | custom-call | tf_op jit(solution)/shard_map/attend/pallas_call | solution.py:160
  67.4 8.5 %collective-permute-done.6 = bf16[256,768]{0,1:T(8,128)(2,1)S(1)} collective-permute-done((bf16[256,768]{0,1:T(8,128)(2,1)S(1)}, bf16[256,768]{0,1:T(8,128)(2,1)S(1)}, u32[]{:S(2)}, u32[]{:S(2)}) %collective-permute-start.6) | collective-permute-done | bytes 393248 | tf_op jit(solution)/shard_map/ppermute | solution.py:33
  75.9 8.7 %collective-permute-done.8 = bf16[256,768]{0,1:T(8,128)(2,1)S(1)} collective-permute-done((bf16[256,768]{0,1:T(8,128)(2,1)S(1)}, bf16[256,768]{0,1:T(8,128)(2,1)S(1)}, u32[]{:S(2)}, u32[]{:S(2)}) %collective-permute-start.8) | collective-permute-done | bytes 393248 | tf_op jit(solution)/shard_map/ppermute | solution.py:33
  90.8 9.4 %collective-permute-done.11 = bf16[256,768]{0,1:T(8,128)(2,1)S(1)} collective-permute-done((bf16[256,768]{0,1:T(8,128)(2,1)S(1)}, bf16[256,768]{0,1:T(8,128)(2,1)S(1)}, u32[]{:S(2)}, u32[]{:S(2)}) %collective-permute-start.11) | collective-permute-done | bytes 393248 | tf_op jit(solution)/shard_map/ppermute | solution.py:33
  100.2 6.3 %collective-permute-done.10 = bf16[256,768]{0,1:T(8,128)(2,1)S(1)} collective-permute-done((bf16[256,768]{0,1:T(8,128)(2,1)S(1)}, bf16[256,768]{0,1:T(8,128)(2,1)S(1)}, u32[]{:S(2)}, u32[]{:S(2)}) %collective-permute-start.10) | collective-permute-done | bytes 393248 | tf_op jit(solution)/shard_map/ppermute | solution.py:33
  118.5 8.5 %collective-permute-done.12 = bf16[256,768]{0,1:T(8,128)(2,1)S(1)} collective-permute-done((bf16[256,768]{0,1:T(8,128)(2,1)S(1)}, bf16[256,768]{0,1:T(8,128)(2,1)S(1)}, u32[]{:S(2)}, u32[]{:S(2)}) %collective-permute-start.12) | collective-permute-done | bytes 393248 | tf_op jit(solution)/shard_map/ppermute | solution.py:33
  127.0 7.7 %collective-permute-done.14 = bf16[256,768]{0,1:T(8,128)(2,1)S(1)} collective-permute-done((bf16[256,768]{0,1:T(8,128)(2,1)S(1)}, bf16[256,768]{0,1:T(8,128)(2,1)S(1)}, u32[]{:S(2)}, u32[]{:S(2)}) %collective-permute-start.14) | collective-permute-done | bytes 393248 | tf_op jit(solution)/shard_map/ppermute | solution.py:33
  141.7 8.0 %collective-permute-done.17 = bf16[256,768]{0,1:T(8,128)(2,1)S(1)} collective-permute-done((bf16[256,768]{0,1:T(8,128)(2,1)S(1)}, bf16[256,768]{0,1:T(8,128)(2,1)S(1)}, u32[]{:S(2)}, u32[]{:S(2)}) %collective-permute-start.17) | collective-permute-done | bytes 393248 | tf_op jit(solution)/shard_map/ppermute | solution.py:33
  159.5 17.4 %attend.3 = (bf16[3,1024,64]{2,1,0:T(8,128)(2,1)}, bf16[3,1024,64]{2,1,0:T(8,128)(2,1)}, bf16[3,1024,64]{2,1,0:T(8,128)(2,1)}, bf16[1024,192]{1,0:T(8,128)(2,1)}, f32[3,8,1024]{2,1,0:T(8,128)}) custom-call(s32[2]{0:T(128)} %pad_add_fusion.scalars, f32[1024,576]{1,0:T(8,128)} %fusion.35.qkv, f32[1024,64]{1,0:T(8,128)} %get-tuple-element.152.cosine, ...), custom_call_target="tpu_custom_call" | custom-call | tf_op jit(solution)/shard_map/attend/pallas_call | solution.py:160
  182.4 8.5 %collective-permute-done.18 = bf16[256,768]{0,1:T(8,128)(2,1)S(1)} collective-permute-done((bf16[256,768]{0,1:T(8,128)(2,1)S(1)}, bf16[256,768]{0,1:T(8,128)(2,1)S(1)}, u32[]{:S(2)}, u32[]{:S(2)}) %collective-permute-start.18) | collective-permute-done | bytes 393248 | tf_op jit(solution)/shard_map/ppermute | solution.py:33
  190.9 8.3 %collective-permute-done.20 = bf16[256,768]{0,1:T(8,128)(2,1)S(1)} collective-permute-done((bf16[256,768]{0,1:T(8,128)(2,1)S(1)}, bf16[256,768]{0,1:T(8,128)(2,1)S(1)}, u32[]{:S(2)}, u32[]{:S(2)}) %collective-permute-start.20) | collective-permute-done | bytes 393248 | tf_op jit(solution)/shard_map/ppermute | solution.py:33
  207.0 7.2 %collective-permute-done.23 = bf16[256,768]{0,1:T(8,128)(2,1)} collective-permute-done((bf16[256,768]{0,1:T(8,128)(2,1)S(1)}, bf16[256,768]{0,1:T(8,128)(2,1)}, u32[]{:S(2)}, u32[]{:S(2)}) %collective-permute-start.23) | collective-permute-done | bytes 393248 | tf_op jit(solution)/shard_map/ppermute | solution.py:33
  214.7 8.0 %collective-permute-done.22 = bf16[256,768]{0,1:T(8,128)(2,1)} collective-permute-done((bf16[256,768]{0,1:T(8,128)(2,1)S(1)}, bf16[256,768]{0,1:T(8,128)(2,1)}, u32[]{:S(2)}, u32[]{:S(2)}) %collective-permute-start.22) | collective-permute-done | bytes 393248 | tf_op jit(solution)/shard_map/ppermute | solution.py:33
  250.5 6.5 %collective-permute-done.31 = bf16[256,768]{0,1:T(8,128)(2,1)S(1)} collective-permute-done((bf16[256,768]{0,1:T(8,128)(2,1)}, bf16[256,768]{0,1:T(8,128)(2,1)S(1)}, u32[]{:S(2)}, u32[]{:S(2)}) %collective-permute-start.31) | collective-permute-done | bytes 393248 | tf_op jit(solution)/shard_map/ppermute | solution.py:33
  257.0 7.7 %collective-permute-done.33 = bf16[256,768]{0,1:T(8,128)(2,1)S(1)} collective-permute-done((bf16[256,768]{0,1:T(8,128)(2,1)}, bf16[256,768]{0,1:T(8,128)(2,1)S(1)}, u32[]{:S(2)}, u32[]{:S(2)}) %collective-permute-start.33) | collective-permute-done | bytes 393248 | tf_op jit(solution)/shard_map/ppermute | solution.py:33
  292.5 21.8 %attend_back.2 = bf16[1024,576]{1,0:T(8,128)(2,1)} custom-call(s32[2]{0:T(128)} %pad_add_fusion.scalars, bf16[3,1024,64]{2,1,0:T(8,128)(2,1)} %get-tuple-element.27.q3, bf16[3,1024,64]{2,1,0:T(8,128)(2,1)} %get-tuple-element.28.k3, bf16[3,1024,64]{2,1,0:T(8,128)(2,1)} %get-tuple-element.29.v3, bf16[1024,192]{1,0:T(8,128)(2,1)} %copy.68.grad, ...), custom_call_target="tpu_custom_call" | custom-call | tf_op jit(solution)/shard_map/attend_back/pallas_call | solution.py:246
  329.6 8.3 %collective-permute-done.39 = bf16[256,768]{0,1:T(8,128)(2,1)S(1)} collective-permute-done((bf16[256,768]{0,1:T(8,128)(2,1)S(1)}, bf16[256,768]{0,1:T(8,128)(2,1)S(1)}, u32[]{:S(2)}, u32[]{:S(2)}) %collective-permute-start.39) | collective-permute-done | bytes 393248 | tf_op jit(solution)/shard_map/ppermute | solution.py:33
  376.3 8.6 %collective-permute-done.45 = bf16[256,768]{0,1:T(8,128)(2,1)S(1)} collective-permute-done((bf16[256,768]{0,1:T(8,128)(2,1)S(1)}, bf16[256,768]{0,1:T(8,128)(2,1)S(1)}, u32[]{:S(2)}, u32[]{:S(2)}) %collective-permute-start.45) | collective-permute-done | bytes 393248 | tf_op jit(solution)/shard_map/ppermute | solution.py:33
  396.9 13.4 %collective-permute-done.48 = bf16[256,768]{0,1:T(8,128)(2,1)} collective-permute-done((bf16[256,768]{0,1:T(8,128)(2,1)S(1)}, bf16[256,768]{0,1:T(8,128)(2,1)}, u32[]{:S(2)}, u32[]{:S(2)}) %collective-permute-start.48) | collective-permute-done | bytes 393248 | tf_op jit(solution)/shard_map/ppermute | solution.py:33
  421.0 14.9 %attend_back.3 = bf16[1024,576]{1,0:T(8,128)(2,1)} custom-call(s32[2]{0:T(128)} %pad_add_fusion.scalars, bf16[3,1024,64]{2,1,0:T(8,128)(2,1)} %get-tuple-element.24.q3, bf16[3,1024,64]{2,1,0:T(8,128)(2,1)} %get-tuple-element.25.k3, bf16[3,1024,64]{2,1,0:T(8,128)(2,1)} %get-tuple-element.26.v3, bf16[1024,192]{1,0:T(8,128)(2,1)} %copy.71.grad, ...), custom_call_target="tpu_custom_call" | custom-call | tf_op jit(solution)/shard_map/attend_back/pallas_call | solution.py:246
  451.0 5.7 %collective-permute-done.49 = bf16[256,768]{0,1:T(8,128)(2,1)S(1)} collective-permute-done((bf16[256,768]{0,1:T(8,128)(2,1)S(1)}, bf16[256,768]{0,1:T(8,128)(2,1)S(1)}, u32[]{:S(2)}, u32[]{:S(2)}) %collective-permute-start.49) | collective-permute-done | bytes 393248 | tf_op jit(solution)/shard_map/ppermute | solution.py:33
  456.8 7.0 %collective-permute-done.51 = bf16[256,768]{0,1:T(8,128)(2,1)S(1)} collective-permute-done((bf16[256,768]{0,1:T(8,128)(2,1)S(1)}, bf16[256,768]{0,1:T(8,128)(2,1)S(1)}, u32[]{:S(2)}, u32[]{:S(2)}) %collective-permute-start.51) | collective-permute-done | bytes 393248 | tf_op jit(solution)/shard_map/ppermute | solution.py:33
  490.5 16.2 %reduce-scatter.13.cloned.1.call-done = bf16[192,384]{1,0:T(8,128)(2,1)} async-done(((bf16[1536,384]{1,0:T(8,128)(2,1)}), bf16[192,384]{1,0:T(8,128)(2,1)}) %reduce-scatter.13.cloned.1.call-update) | async-done | bytes 147472
  (438 shorter events, 269.9 us)
Async XLA Ops:
  7.2 37.4 %all-gather.5.cloned.1.call-start = ((), (), s32[]{:S(2)}) async-start(), calls=%async_computation.4 | async-start | bytes 2654208 | tf_op jit(solution)/shard_map/all_gather | solution.py:337
  9.2 81.6 %all-gather.7.cloned.1.call-start = ((), (), s32[]{:S(2)}) async-start(), calls=%async_computation.5 | async-start | bytes 3096576 | tf_op jit(solution)/shard_map/all_gather | solution.py:338
  12.8 470.2 %reduce-scatter.19.cloned.1.call-start = ((), (), s32[]{:S(2)}) async-start(), calls=%async_computation.9 | async-start | bytes 1769472
  65.4 19.2 %collective-permute-start.8 = (bf16[256,768]{0,1:T(8,128)(2,1)S(1)}, bf16[256,768]{0,1:T(8,128)(2,1)S(1)}, u32[]{:S(2)}, u32[]{:S(2)}) collective-permute-start(bf16[256,768]{0,1:T(8,128)(2,1)S(1)} %get-tuple-element.124), channel_id=1, source_target_pairs={{0,3},{1,2},{2,1},{3,0},{4,7},{5,6},{6,5},{7,4},{8,11},{9,10},{10,... | collective-permute-start | bytes 1179656 | tf_op jit(solution)/shard_map/ppermute | solution.py:33
  66.9 19.1 %collective-permute-start.7 = (bf16[256,768]{0,1:T(8,128)(2,1)S(1)}, bf16[256,768]{0,1:T(8,128)(2,1)S(1)}, u32[]{:S(2)}, u32[]{:S(2)}) collective-permute-start(bf16[256,768]{0,1:T(8,128)(2,1)S(1)} %get-tuple-element.125), channel_id=1, source_target_pairs={{0,2},{1,3},{2,0},{3,1},{4,6},{5,7},{6,4},{7,5},{8,10},{9,11},{10,... | collective-permute-start | bytes 1179656 | tf_op jit(solution)/shard_map/ppermute | solution.py:33
  117.0 19.0 %collective-permute-start.13 = (bf16[256,768]{0,1:T(8,128)(2,1)S(1)}, bf16[256,768]{0,1:T(8,128)(2,1)S(1)}, u32[]{:S(2)}, u32[]{:S(2)}) collective-permute-start(bf16[256,768]{0,1:T(8,128)(2,1)S(1)} %get-tuple-element.122), channel_id=1, source_target_pairs={{0,2},{1,3},{2,0},{3,1},{4,6},{5,7},{6,4},{7,5},{8,10},{9,11},{10,... | collective-permute-start | bytes 1179656 | tf_op jit(solution)/shard_map/ppermute | solution.py:33
  202.9 19.8 %collective-permute-start.22 = (bf16[256,768]{0,1:T(8,128)(2,1)S(1)}, bf16[256,768]{0,1:T(8,128)(2,1)}, u32[]{:S(2)}, u32[]{:S(2)}) collective-permute-start(bf16[256,768]{0,1:T(8,128)(2,1)S(1)} %multiply_convert_fusion.4), channel_id=1, source_target_pairs={{0,2},{1,3},{2,0},{3,1},{4,6},{5,7},{6,4},{7,5},{8,10},{9,11},{10,... | collective-permute-start | bytes 1179656 | tf_op jit(solution)/shard_map/ppermute | solution.py:33
  203.2 19.5 %collective-permute-start.21 = (bf16[256,768]{0,1:T(8,128)(2,1)S(1)}, bf16[256,768]{0,1:T(8,128)(2,1)}, u32[]{:S(2)}, u32[]{:S(2)}) collective-permute-start(bf16[256,768]{0,1:T(8,128)(2,1)S(1)} %multiply_convert_fusion.4), channel_id=1, source_target_pairs={{0,1},{1,0},{2,3},{3,2},{4,5},{5,4},{6,7},{7,6},{8,9},{9,8},{10,11... | collective-permute-start | bytes 1179656 | tf_op jit(solution)/shard_map/ppermute | solution.py:33
  205.0 26.0 %collective-permute-start.30 = (bf16[256,768]{0,1:T(8,128)(2,1)S(1)}, bf16[256,768]{0,1:T(8,128)(2,1)S(1)}, u32[]{:S(2)}, u32[]{:S(2)}) collective-permute-start(bf16[256,768]{0,1:T(8,128)(2,1)S(1)} %bitcast.90), channel_id=1, source_target_pairs={{0,3},{1,2},{2,1},{3,0},{4,7},{5,6},{6,5},{7,4},{8,11},{9,10},{10,... | collective-permute-start | bytes 1179656 | tf_op jit(solution)/shard_map/ppermute | solution.py:33
  206.7 29.5 %collective-permute-start.29 = (bf16[256,768]{0,1:T(8,128)(2,1)S(1)}, bf16[256,768]{0,1:T(8,128)(2,1)S(1)}, u32[]{:S(2)}, u32[]{:S(2)}) collective-permute-start(bf16[256,768]{0,1:T(8,128)(2,1)S(1)} %bitcast.91), channel_id=1, source_target_pairs={{0,2},{1,3},{2,0},{3,1},{4,6},{5,7},{6,4},{7,5},{8,10},{9,11},{10,... | collective-permute-start | bytes 1179656 | tf_op jit(solution)/shard_map/ppermute | solution.py:33
  214.2 21.9 %collective-permute-start.28 = (bf16[256,768]{0,1:T(8,128)(2,1)S(1)}, bf16[256,768]{0,1:T(8,128)(2,1)S(1)}, u32[]{:S(2)}, u32[]{:S(2)}) collective-permute-start(bf16[256,768]{0,1:T(8,128)(2,1)S(1)} %bitcast.92), channel_id=1, source_target_pairs={{0,1},{1,0},{2,3},{3,2},{4,5},{5,4},{6,7},{7,6},{8,9},{9,8},{10,11... | collective-permute-start | bytes 1179656 | tf_op jit(solution)/shard_map/ppermute | solution.py:33
  245.7 19.1 %collective-permute-start.33 = (bf16[256,768]{0,1:T(8,128)(2,1)}, bf16[256,768]{0,1:T(8,128)(2,1)S(1)}, u32[]{:S(2)}, u32[]{:S(2)}) collective-permute-start(bf16[256,768]{0,1:T(8,128)(2,1)} %get-tuple-element.112), channel_id=1, source_target_pairs={{0,3},{1,2},{2,1},{3,0},{4,7},{5,6},{6,5},{7,4},{8,11},{9,10},{10,... | collective-permute-start | bytes 1179656 | tf_op jit(solution)/shard_map/ppermute | solution.py:33
  247.0 19.2 %collective-permute-start.32 = (bf16[256,768]{0,1:T(8,128)(2,1)}, bf16[256,768]{0,1:T(8,128)(2,1)}, u32[]{:S(2)}, u32[]{:S(2)}) collective-permute-start(bf16[256,768]{0,1:T(8,128)(2,1)} %get-tuple-element.113), channel_id=1, source_target_pairs={{0,2},{1,3},{2,0},{3,1},{4,6},{5,7},{6,4},{7,5},{8,10},{9,11},{10,... | collective-permute-start | bytes 1179656 | tf_op jit(solution)/shard_map/ppermute | solution.py:33
  280.6 204.9 %reduce-scatter.15.cloned.1.call-start = ((), (), s32[]{:S(2)}) async-start(), calls=%async_computation.7 | async-start | bytes 1327104
  349.5 137.1 %reduce-scatter.17.cloned.1.call-start = ((), (), s32[]{:S(2)}) async-start(), calls=%async_computation.8 | async-start | bytes 1769472
  365.2 19.7 %collective-permute-start.45 = (bf16[256,768]{0,1:T(8,128)(2,1)S(1)}, bf16[256,768]{0,1:T(8,128)(2,1)S(1)}, u32[]{:S(2)}, u32[]{:S(2)}) collective-permute-start(bf16[256,768]{0,1:T(8,128)(2,1)S(1)} %get-tuple-element.106), channel_id=1, source_target_pairs={{0,3},{1,2},{2,1},{3,0},{4,7},{5,6},{6,5},{7,4},{8,11},{9,10},{10,... | collective-permute-start | bytes 1179656 | tf_op jit(solution)/shard_map/ppermute | solution.py:33
  368.9 78.3 %collective-permute-start.24 = (bf16[256,768]{0,1:T(8,128)(2,1)}, bf16[256,768]{0,1:T(8,128)(2,1)}, u32[]{:S(2)}, u32[]{:S(2)}) collective-permute-start(bf16[256,768]{0,1:T(8,128)(2,1)} %get-tuple-element.114), channel_id=1, source_target_pairs={{0,1},{1,0},{2,3},{3,2},{4,5},{5,4},{6,7},{7,6},{8,9},{9,8},{10,11... | collective-permute-start | bytes 1179656 | tf_op jit(solution)/shard_map/ppermute | solution.py:33
  369.8 78.5 %collective-permute-start.26 = (bf16[256,768]{0,1:T(8,128)(2,1)}, bf16[256,768]{0,1:T(8,128)(2,1)}, u32[]{:S(2)}, u32[]{:S(2)}) collective-permute-start(bf16[256,768]{0,1:T(8,128)(2,1)} %get-tuple-element.115), channel_id=1, source_target_pairs={{0,3},{1,2},{2,1},{3,0},{4,7},{5,6},{6,5},{7,4},{8,11},{9,10},{10,... | collective-permute-start | bytes 1179656 | tf_op jit(solution)/shard_map/ppermute | solution.py:33
  387.1 23.2 %collective-permute-start.48 = (bf16[256,768]{0,1:T(8,128)(2,1)S(1)}, bf16[256,768]{0,1:T(8,128)(2,1)}, u32[]{:S(2)}, u32[]{:S(2)}) collective-permute-start(bf16[256,768]{0,1:T(8,128)(2,1)S(1)} %fusion.58), channel_id=1, source_target_pairs={{0,3},{1,2},{2,1},{3,0},{4,7},{5,6},{6,5},{7,4},{8,11},{9,10},{10,... | collective-permute-start | bytes 1179656 | tf_op jit(solution)/shard_map/ppermute | solution.py:33
  388.4 28.2 %collective-permute-start.47 = (bf16[256,768]{0,1:T(8,128)(2,1)S(1)}, bf16[256,768]{0,1:T(8,128)(2,1)}, u32[]{:S(2)}, u32[]{:S(2)}) collective-permute-start(bf16[256,768]{0,1:T(8,128)(2,1)S(1)} %fusion.58), channel_id=1, source_target_pairs={{0,2},{1,3},{2,0},{3,1},{4,6},{5,7},{6,4},{7,5},{8,10},{9,11},{10,... | collective-permute-start | bytes 1179656 | tf_op jit(solution)/shard_map/ppermute | solution.py:33
  390.1 27.6 %collective-permute-start.46 = (bf16[256,768]{0,1:T(8,128)(2,1)S(1)}, bf16[256,768]{0,1:T(8,128)(2,1)}, u32[]{:S(2)}, u32[]{:S(2)}) collective-permute-start(bf16[256,768]{0,1:T(8,128)(2,1)S(1)} %fusion.58), channel_id=1, source_target_pairs={{0,1},{1,0},{2,3},{3,2},{4,5},{5,4},{6,7},{7,6},{8,9},{9,8},{10,11... | collective-permute-start | bytes 1179656 | tf_op jit(solution)/shard_map/ppermute | solution.py:33
  396.7 110.0 %reduce-scatter.13.cloned.1.call-start = ((), (), s32[]{:S(2)}) async-start(), calls=%async_computation.6 | async-start | bytes 1327104
  410.3 38.0 %collective-permute-start.25 = (bf16[256,768]{0,1:T(8,128)(2,1)S(1)}, bf16[256,768]{0,1:T(8,128)(2,1)}, u32[]{:S(2)}, u32[]{:S(2)}) collective-permute-start(bf16[256,768]{0,1:T(8,128)(2,1)S(1)} %copy-done.22), channel_id=1, source_target_pairs={{0,2},{1,3},{2,0},{3,1},{4,6},{5,7},{6,4},{7,5},{8,10},{9,11},{10,... | collective-permute-start | bytes 1179656 | tf_op jit(solution)/shard_map/ppermute | solution.py:33
  450.8 20.8 %collective-permute-start.27 = (bf16[256,768]{0,1:T(8,128)(2,1)}, bf16[256,768]{0,1:T(8,128)(2,1)}, u32[]{:S(2)}, u32[]{:S(2)}) collective-permute-start(bf16[256,768]{0,1:T(8,128)(2,1)} %get-tuple-element.88), channel_id=1, source_target_pairs={{0,16},{16,0},{1,17},{17,1},{2,18},{18,2},{3,19},{19,3},{4,20},{20... | collective-permute-start | bytes 1179656 | tf_op jit(solution)/shard_map/ppermute | solution.py:401
  (128 other events, 1381.1 us)
Sparse Core Ops, SparseCore 0:
  10.2 34.4 all-gather.4
  46.2 34.1 all-gather.6
  280.7 37.9 reduce-scatter.18
  349.6 35.2 reduce-scatter.14
  396.8 37.8 reduce-scatter.16
  471.3 35.3 reduce-scatter.12
